TPU v7x, 1024 devices: a whole 4x8x16 slice. The times are simulated.
1024 devices in a mesh: leaf: 16 (over z_lo, core), head: 64 (over z_hi, y, x).
Axes of the slice: x: 4, y: 8, z: 16 (z_hi: 2, z_lo: 8; z = z_hi * 8 + z_lo), core: 2. Of those that a mesh axis runs over, the one named last changes fastest.
Arguments:
- leaf_query: bfloat16 [16384, 8192], P('leaf', 'head'), may hold values from -6 to 6
- leaf_keys: bfloat16 [16384, 8192], P('leaf', 'head'), may hold values from -6 to 6
- leaf_values: bfloat16 [16384, 8192], P('leaf', 'head'), may hold values from -6 to 6
- out_grad: bfloat16 [16384, 8192], P('leaf', 'head'), may hold values from -6 to 6
- leaf_len: int32 [16], P('leaf'), may hold values from 1 to 1024, 12288 in all
- branch_id: int32 [16], P('leaf'), may hold values from 0 to 1
- trunk_keys: bfloat16 [8192, 8192], P('leaf', 'head'), may hold values from -6 to 6
- trunk_values: bfloat16 [8192, 8192], P('leaf', 'head'), may hold values from -6 to 6
- branch_keys: bfloat16 [8192, 8192], P('leaf', 'head'), may hold values from -6 to 6
- branch_values: bfloat16 [8192, 8192], P('leaf', 'head'), may hold values from -6 to 6
- norm_gain: bfloat16 [8192], P('head'), may hold values from 0.099609375 to 1.8984375
Outputs:
- leaf_out: bfloat16 [16384, 8192], P('leaf', 'head')
- query_grad: bfloat16 [16384, 8192], P('leaf', 'head')
- key_grad: bfloat16 [16384, 8192], P('leaf', 'head')
- value_grad: bfloat16 [16384, 8192], P('leaf', 'head')
- trunk_key_grad: bfloat16 [8192, 8192], P('leaf', 'head')
- trunk_value_grad: bfloat16 [8192, 8192], P('leaf', 'head')
- branch_key_grad: bfloat16 [8192, 8192], P('leaf', 'head')
- branch_value_grad: bfloat16 [8192, 8192], P('leaf', 'head')
Inputs may be any that keep to these rules, and one draw needn't show every extreme that they name: `leaf_len`: A leaf's live slots are its first ones; the longest leaf has exactly 1024.
All inputs are finite; a program needn't handle non-finite values. No bound on the sum of `leaf_len` on one device may be relied on, other than what follows from the above.
Results may differ from a plain program's by a relative error of at most 0.0058.
Values sent between devices are 32-bit elements; how exact they have to be, the bound alone decides.
No kernel may reach another device: no remote copies, remote signals or barrier semaphores. Data moves between devices by JAX's collectives and lax.ppermute only.
A program may use at most 32 MiB of HBM per device.

v0:
```python
import jax
import jax.numpy as jnp
from jax import lax
from jax.sharding import PartitionSpec as P

DH = 128
BLOCK = 512


epsilon = 1e-06
highest = lax.Precision.HIGHEST


def from_partner(value, axis, bit):
    mask = 2**bit
    pairs = [(source, source ^ mask) for source in range(lax.axis_size(axis))]
    return lax.ppermute(value, axis, pairs)


def sent_to_all(value, axis):
    count = lax.axis_size(axis)
    return lax.all_to_all(
        jnp.broadcast_to(value[None], (count, *value.shape)), axis, 0, 0, tiled=True
    )


def over_copies(value, axis):
    everything = sent_to_all(value, axis)
    return jnp.sum(everything, axis=0)


def shards(
    leaf_query,
    leaf_keys,
    leaf_values,
    out_grad,
    leaf_len,
    branch_id,
    trunk_keys,
    trunk_values,
    branch_keys,
    branch_values,
    norm_gain,
):
    row_count, row_width = leaf_query.shape
    head_count = row_width // DH
    block_count = row_count // BLOCK
    trunk_k = trunk_keys.reshape(-1, head_count, DH)
    trunk_v = trunk_values.reshape(-1, head_count, DH)
    branch_k = branch_keys.reshape(-1, head_count, DH)
    branch_v = branch_values.reshape(-1, head_count, DH)
    trunk_part = jnp.einsum("thd,the->hde", trunk_k, trunk_v, preferred_element_type=jnp.float32)
    branch_part = jnp.einsum("thd,the->hde", branch_k, branch_v, preferred_element_type=jnp.float32)
    leaf_count = lax.axis_size("leaf")
    upper_half = lax.axis_index("leaf") >= leaf_count // 2
    first_branch = branch_id[0] == 0
    paired = jnp.stack([trunk_part, branch_part])
    top_bit = leaf_count.bit_length() - 2
    for level_bit in range(top_bit):
        paired = paired + from_partner(paired, "leaf", level_bit)
    across = from_partner(paired, "leaf", top_bit)
    trunk_total = paired[0] + across[0]
    branch_total = jnp.where(
        upper_half, jnp.stack([across[1], paired[1]]), jnp.stack([paired[1], across[1]])
    )
    prefix_state = trunk_total + jnp.where(first_branch, branch_total[0], branch_total[1])
    live_rows = (jnp.arange(row_count, dtype=jnp.int32) < leaf_len[0]).astype(jnp.float32)
    keep_mask = live_rows.astype(jnp.bfloat16)[:, None]

    def to_blocks(values):
        return values.reshape(block_count, BLOCK, head_count, DH)

    queries = to_blocks(leaf_query)
    keys_masked = to_blocks(leaf_keys * keep_mask)
    values_masked = to_blocks(leaf_values * keep_mask)
    block_sums = jnp.einsum(
        "jthd,jthe->jhde", keys_masked, values_masked, preferred_element_type=jnp.float32
    )
    earlier = jnp.concatenate(
        [jnp.zeros_like(block_sums[:1]), jnp.cumsum(block_sums, axis=0)[:-1]], axis=0
    )
    states = (prefix_state[None] + earlier).astype(jnp.bfloat16)
    causal = jnp.tril(jnp.ones((BLOCK, BLOCK), jnp.float32))
    mixing = (
        jnp.einsum("jqhd,jkhd->jhqk", queries, keys_masked, preferred_element_type=jnp.float32)
        * causal
    ).astype(jnp.bfloat16)
    raw_out = jnp.einsum(
        "jqhd,jhde->jqhe", queries, states, preferred_element_type=jnp.float32
    ) + jnp.einsum("jhqk,jkhe->jqhe", mixing, values_masked, preferred_element_type=jnp.float32)
    raw_out = raw_out.reshape(row_count, row_width) * live_rows[:, None]
    features = row_width * lax.axis_size("head")
    square_sum = over_copies(jnp.sum(raw_out * raw_out, axis=1), "head")
    norm_scale = lax.rsqrt(square_sum / features + epsilon)
    gain_values = norm_gain.astype(jnp.float32)
    leaf_out = (raw_out * norm_scale[:, None] * gain_values).astype(jnp.bfloat16)
    scaled_grad = out_grad.astype(jnp.float32) * gain_values
    inner_sum = over_copies(jnp.sum(raw_out * scaled_grad, axis=1), "head")
    raw_grad = (
        norm_scale[:, None] * scaled_grad
        - raw_out * (norm_scale**3 * inner_sum / features)[:, None]
    ) * live_rows[:, None]
    raw_grad = to_blocks(raw_grad.astype(jnp.bfloat16))
    prob_grad = (
        jnp.einsum("jqhe,jkhe->jhqk", raw_grad, values_masked, preferred_element_type=jnp.float32)
        * causal
    ).astype(jnp.bfloat16)
    block_grads = jnp.einsum(
        "jqhd,jqhe->jhde", queries, raw_grad, preferred_element_type=jnp.float32
    )
    prefix_grad = jnp.sum(block_grads, axis=0)
    grad_slots = jnp.stack(
        [jnp.where(first_branch, prefix_grad, 0.0), jnp.where(first_branch, 0.0, prefix_grad)]
    )
    branch_sums = over_copies(grad_slots, "leaf")
    trunk_sum = branch_sums[0] + branch_sums[1]
    query_grad = jnp.einsum(
        "jqhe,jhde->jqhd", raw_grad, states, preferred_element_type=jnp.float32
    ) + jnp.einsum("jhqk,jkhd->jqhd", prob_grad, keys_masked, preferred_element_type=jnp.float32)
    reverse_sums = jnp.cumsum(block_grads[::-1], axis=0)[::-1]
    later_sums = jnp.concatenate(
        [reverse_sums[1:], jnp.zeros_like(block_grads[:1])], axis=0
    ).astype(jnp.bfloat16)
    key_grad = jnp.einsum(
        "jhqk,jqhd->jkhd", prob_grad, queries, preferred_element_type=jnp.float32
    ) + jnp.einsum("jkhe,jhde->jkhd", values_masked, later_sums, preferred_element_type=jnp.float32)
    value_grad = jnp.einsum(
        "jhqk,jqhe->jkhe", mixing, raw_grad, preferred_element_type=jnp.float32
    ) + jnp.einsum("jkhd,jhde->jkhe", keys_masked, later_sums, preferred_element_type=jnp.float32)
    own_grad = jnp.where(upper_half, branch_sums[1], branch_sums[0])
    trunk_kf = trunk_k.astype(jnp.float32)
    trunk_vf = trunk_v.astype(jnp.float32)
    branch_kf = branch_k.astype(jnp.float32)
    branch_vf = branch_v.astype(jnp.float32)
    trunk_key_grad = jnp.einsum("the,hde->thd", trunk_vf, trunk_sum, precision=highest)
    trunk_value_grad = jnp.einsum("thd,hde->the", trunk_kf, trunk_sum, precision=highest)
    branch_key_grad = jnp.einsum("the,hde->thd", branch_vf, own_grad, precision=highest)
    branch_value_grad = jnp.einsum("thd,hde->the", branch_kf, own_grad, precision=highest)
    return (
        leaf_out,
        query_grad.reshape(row_count, row_width).astype(jnp.bfloat16),
        key_grad.reshape(row_count, row_width).astype(jnp.bfloat16),
        value_grad.reshape(row_count, row_width).astype(jnp.bfloat16),
        trunk_key_grad.reshape(-1, row_width).astype(jnp.bfloat16),
        trunk_value_grad.reshape(-1, row_width).astype(jnp.bfloat16),
        branch_key_grad.reshape(-1, row_width).astype(jnp.bfloat16),
        branch_value_grad.reshape(-1, row_width).astype(jnp.bfloat16),
    )


def solution(mesh):
    placed = (
        P("leaf", "head"),
        P("leaf", "head"),
        P("leaf", "head"),
        P("leaf", "head"),
        P("leaf"),
        P("leaf"),
        P("leaf", "head"),
        P("leaf", "head"),
        P("leaf", "head"),
        P("leaf", "head"),
        P("head"),
    )
    return jax.shard_map(
        shards,
        mesh=mesh,
        in_specs=placed,
        out_specs=(
            P("leaf", "head"),
            P("leaf", "head"),
            P("leaf", "head"),
            P("leaf", "head"),
            P("leaf", "head"),
            P("leaf", "head"),
            P("leaf", "head"),
            P("leaf", "head"),
        ),
        check_vma=False,
    )
```

profile of v0, /device:TPU:193, one launch (start us, length us, event | category | flops | bytes accessed | tf_op | source)
XLA Modules:
  0.0 234.7 jit_solution(8064683714990577246)
XLA Ops:
  0.6 1.2 convolution_bitcast_fusion.4
  1.9 1.2 convolution_bitcast_fusion.3
  3.1 2.6 %collective-permute-start = (f32[2,1,128,128]{3,2,1,0:T(8,128)S(1)}, f32[2,1,128,128]{3,2,1,0:T(8,128)S(1)}, u32[]{:S(2)}, u32[]{:S(2)}) collective-permute-start(f32[2,1,128,128]{3,2,1,0:T(8,128)S(1)} %pad_maximum_fusion), channel_id=1, source_target_pairs={{0,64},{64,0},{128,192},{192,128},{256,320},{320,256},{384,448},{4... | collective-permute-start | bytes 393224 | tf_op jit(solution)/shard_map/ppermute | solution.py:17
  6.4 1.2 broadcast_multiply_fusion
  7.8 1.9 collective-permute-start.1
  9.7 0.4 fusion
  10.2 4.5 %collective-permute-done.1 = f32[2,1,128,128]{3,2,1,0:T(8,128)S(1)} collective-permute-done((f32[2,1,128,128]{3,2,1,0:T(8,128)S(1)}, f32[2,1,128,128]{3,2,1,0:T(8,128)S(1)}, u32[]{:S(2)}, u32[]{:S(2)}) %collective-permute-start.1) | collective-permute-done | bytes 131104 | tf_op jit(solution)/shard_map/ppermute | solution.py:17
  14.7 11.2 %collective-permute-start.2 = (f32[2,1,128,128]{3,2,1,0:T(8,128)S(1)}, f32[2,1,128,128]{3,2,1,0:T(8,128)S(1)}, u32[]{:S(2)}, u32[]{:S(2)}) collective-permute-start(f32[2,1,128,128]{3,2,1,0:T(8,128)S(1)} %fusion.68), channel_id=1, source_target_pairs={{0,256},{64,320},{128,384},{192,448},{256,0},{320,64},{384,128},{4... | collective-permute-start | bytes 393224 | tf_op jit(solution)/shard_map/ppermute | solution.py:17
  25.9 0.3 convolution_bitcast_fusion.2
  26.2 5.8 %collective-permute-done.2 = f32[2,1,128,128]{3,2,1,0:T(8,128)S(1)} collective-permute-done((f32[2,1,128,128]{3,2,1,0:T(8,128)S(1)}, f32[2,1,128,128]{3,2,1,0:T(8,128)S(1)}, u32[]{:S(2)}, u32[]{:S(2)}) %collective-permute-start.2) | collective-permute-done | bytes 131104 | tf_op jit(solution)/shard_map/ppermute | solution.py:17
  32.0 4.4 %collective-permute-start.3 = (f32[2,1,128,128]{3,2,1,0:T(8,128)S(1)}, f32[2,1,128,128]{3,2,1,0:T(8,128)S(1)}, u32[]{:S(2)}, u32[]{:S(2)}) collective-permute-start(f32[2,1,128,128]{3,2,1,0:T(8,128)S(1)} %add.88), channel_id=1, source_target_pairs={{0,512},{64,576},{128,640},{192,704},{256,768},{320,832},{384,896}... | collective-permute-start | bytes 393224 | tf_op jit(solution)/shard_map/ppermute | solution.py:17
  37.2 9.2 %collective-permute-done.3 = f32[2,1,128,128]{3,2,1,0:T(8,128)S(1)} collective-permute-done((f32[2,1,128,128]{3,2,1,0:T(8,128)S(1)}, f32[2,1,128,128]{3,2,1,0:T(8,128)S(1)}, u32[]{:S(2)}, u32[]{:S(2)}) %collective-permute-start.3) | collective-permute-done | bytes 131104 | tf_op jit(solution)/shard_map/ppermute | solution.py:17
  46.4 0.3 fusion.23
  46.7 1.2 multiply_reduce_fusion.1
  47.9 0.8 broadcast_in_dim.24
  48.7 18.2 %all-to-all-start = ((f32[64,1,1024]{2,1,0:T(1,128)}), f32[64,1,1024]{2,1,0:T(1,128)S(1)}, u32[]{:S(2)}, u32[]{:S(2)}) async-start(f32[64,1,1024]{2,1,0:T(1,128)} %broadcast_in_dim.24), calls=%async_computation | async-start | bytes 524288 | tf_op jit(solution)/shard_map/all_to_all | solution.py:22
  66.9 1.2 copy.98
  68.2 0.4 multiply_reduce_fusion
  68.5 20.1 %all-to-all-done = f32[64,1,1024]{2,1,0:T(1,128)S(1)} async-done(((f32[64,1,1024]{2,1,0:T(1,128)}), f32[64,1,1024]{2,1,0:T(1,128)S(1)}, u32[]{:S(2)}, u32[]{:S(2)}) %all-to-all-start) | async-done | bytes 262176 | tf_op jit(solution)/shard_map/all_to_all | solution.py:22
  88.7 0.8 broadcast_in_dim.26
  89.5 5.5 %all-to-all-start.1 = ((f32[64,1,1024]{2,1,0:T(1,128)}), f32[64,1,1024]{2,1,0:T(1,128)}, u32[]{:S(2)}, u32[]{:S(2)}) async-start(f32[64,1,1024]{2,1,0:T(1,128)} %broadcast_in_dim.26), calls=%async_computation.1 | async-start | bytes 524288 | tf_op jit(solution)/shard_map/all_to_all | solution.py:22
  95.0 0.2 reduce_sum.55
  95.2 21.5 %all-to-all-done.1 = f32[64,1,1024]{2,1,0:T(1,128)} async-done(((f32[64,1,1024]{2,1,0:T(1,128)}), f32[64,1,1024]{2,1,0:T(1,128)}, u32[]{:S(2)}, u32[]{:S(2)}) %all-to-all-start.1) | async-done | bytes 262176 | tf_op jit(solution)/shard_map/all_to_all | solution.py:22
  116.7 1.1 reduce_sum.57
  117.9 1.2 multiply_convert_fusion.1
  119.1 0.3 fusion.32
  119.5 1.5 broadcast_in_dim.29
  121.0 14.0 %all-to-all-start.2 = ((f32[16,2,1,128,128]{4,3,2,1,0:T(8,128)}), f32[16,2,1,128,128]{4,3,2,1,0:T(8,128)}, u32[]{:S(2)}, u32[]{:S(2)}) async-start(f32[16,2,1,128,128]{4,3,2,1,0:T(8,128)} %broadcast_in_dim.29), calls=%async_computation.2 | async-start | bytes 4194304 | tf_op jit(solution)/shard_map/all_to_all | solution.py:22
  135.1 0.7 reduce_window_sum.20
  135.7 0.2 fusion.21
  136.0 1.5 multiply_convert_fusion
  137.5 1.4 fusion.7
  138.9 0.8 copy.104
  139.8 0.2 fusion.34
  140.1 0.5 fusion.6
  140.6 0.8 copy.110
  141.4 0.2 fusion.35
  141.7 1.1 fusion.3
  142.8 85.9 %all-to-all-done.2 = f32[16,2,1,128,128]{4,3,2,1,0:T(8,128)} async-done(((f32[16,2,1,128,128]{4,3,2,1,0:T(8,128)}), f32[16,2,1,128,128]{4,3,2,1,0:T(8,128)}, u32[]{:S(2)}, u32[]{:S(2)}) %all-to-all-start.2) | async-done | bytes 2097184 | tf_op jit(solution)/shard_map/all_to_all | solution.py:22
  228.7 1.7 reduce_sum.59
  230.4 0.3 fusion.11
  230.8 0.3 fusion.10
  231.1 0.3 fusion.9
  231.4 0.3 fusion.8
  231.7 0.8 copy.115
  232.4 0.8 copy.114
  233.2 0.8 copy.112
  234.0 0.8 copy.113
  (51 shorter events, 0.6 us)
Async XLA Ops:
  0.6 9.1 %copy-start = (bf16[1024,128]{1,0:T(8,128)(2,1)S(1)}, bf16[1024,128]{1,0:T(8,128)(2,1)}, u32[]{:S(2)}) copy-start(bf16[1024,128]{1,0:T(8,128)(2,1)} %param.11) | copy-start | bytes 786436
  3.1 4.6 %collective-permute-start = (f32[2,1,128,128]{3,2,1,0:T(8,128)S(1)}, f32[2,1,128,128]{3,2,1,0:T(8,128)S(1)}, u32[]{:S(2)}, u32[]{:S(2)}) collective-permute-start(f32[2,1,128,128]{3,2,1,0:T(8,128)S(1)} %pad_maximum_fusion), channel_id=1, source_target_pairs={{0,64},{64,0},{128,192},{192,128},{256,320},{320,256},{384,448},{4... | collective-permute-start | bytes 393224 | tf_op jit(solution)/shard_map/ppermute | solution.py:17
  7.6 18.3 %copy-start.5 = (bf16[1024,128]{1,0:T(8,128)(2,1)}, bf16[1024,128]{1,0:T(8,128)(2,1)S(1)}, u32[]{:S(2)}) copy-start(bf16[1024,128]{1,0:T(8,128)(2,1)S(1)} %get-tuple-element.55) | copy-start | bytes 786436
  7.6 39.1 %copy-start.1 = (bf16[1024,128]{1,0:T(8,128)(2,1)}, bf16[1024,128]{1,0:T(8,128)(2,1)S(1)}, u32[]{:S(2)}) copy-start(bf16[1024,128]{1,0:T(8,128)(2,1)S(1)} %get-tuple-element.54) | copy-start | bytes 786436
  7.8 6.9 %collective-permute-start.1 = (f32[2,1,128,128]{3,2,1,0:T(8,128)S(1)}, f32[2,1,128,128]{3,2,1,0:T(8,128)S(1)}, u32[]{:S(2)}, u32[]{:S(2)}) collective-permute-start(f32[2,1,128,128]{3,2,1,0:T(8,128)S(1)} %fusion.31), channel_id=1, source_target_pairs={{0,128},{64,192},{128,0},{192,64},{256,384},{320,448},{384,256},{4... | collective-permute-start | bytes 393224 | tf_op jit(solution)/shard_map/ppermute | solution.py:17
  14.7 17.3 %collective-permute-start.2 = (f32[2,1,128,128]{3,2,1,0:T(8,128)S(1)}, f32[2,1,128,128]{3,2,1,0:T(8,128)S(1)}, u32[]{:S(2)}, u32[]{:S(2)}) collective-permute-start(f32[2,1,128,128]{3,2,1,0:T(8,128)S(1)} %fusion.68), channel_id=1, source_target_pairs={{0,256},{64,320},{128,384},{192,448},{256,0},{320,64},{384,128},{4... | collective-permute-start | bytes 393224 | tf_op jit(solution)/shard_map/ppermute | solution.py:17
  32.0 14.4 %collective-permute-start.3 = (f32[2,1,128,128]{3,2,1,0:T(8,128)S(1)}, f32[2,1,128,128]{3,2,1,0:T(8,128)S(1)}, u32[]{:S(2)}, u32[]{:S(2)}) collective-permute-start(f32[2,1,128,128]{3,2,1,0:T(8,128)S(1)} %add.88), channel_id=1, source_target_pairs={{0,512},{64,576},{128,640},{192,704},{256,768},{320,832},{384,896}... | collective-permute-start | bytes 393224 | tf_op jit(solution)/shard_map/ppermute | solution.py:17
  46.4 20.5 %copy-start.14 = (bf16[128]{0:T(256)(128)(2,1)S(1)}, bf16[128]{0:T(256)(128)(2,1)}, u32[]{:S(2)}) copy-start(bf16[128]{0:T(256)(128)(2,1)} %param.21) | copy-start | bytes 772
  46.7 21.4 %copy-start.7 = (bf16[1024,128]{1,0:T(8,128)(2,1)S(1)}, bf16[1024,128]{1,0:T(8,128)(2,1)}, u32[]{:S(2)}) copy-start(bf16[1024,128]{1,0:T(8,128)(2,1)} %param.14) | copy-start | bytes 786436
  48.7 39.9 %all-to-all-start = ((f32[64,1,1024]{2,1,0:T(1,128)}), f32[64,1,1024]{2,1,0:T(1,128)S(1)}, u32[]{:S(2)}, u32[]{:S(2)}) async-start(f32[64,1,1024]{2,1,0:T(1,128)} %broadcast_in_dim.24), calls=%async_computation | async-start | bytes 524288 | tf_op jit(solution)/shard_map/all_to_all | solution.py:22
  89.5 27.2 %all-to-all-start.1 = ((f32[64,1,1024]{2,1,0:T(1,128)}), f32[64,1,1024]{2,1,0:T(1,128)}, u32[]{:S(2)}, u32[]{:S(2)}) async-start(f32[64,1,1024]{2,1,0:T(1,128)} %broadcast_in_dim.26), calls=%async_computation.1 | async-start | bytes 524288 | tf_op jit(solution)/shard_map/all_to_all | solution.py:22
  119.1 16.7 %copy-start.3 = (bf16[1024,128]{1,0:T(8,128)(2,1)}, bf16[1024,128]{1,0:T(8,128)(2,1)S(1)}, u32[]{:S(2)}) copy-start(bf16[1024,128]{1,0:T(8,128)(2,1)S(1)} %get-tuple-element.48) | copy-start | bytes 786436
  121.0 107.7 %all-to-all-start.2 = ((f32[16,2,1,128,128]{4,3,2,1,0:T(8,128)}), f32[16,2,1,128,128]{4,3,2,1,0:T(8,128)}, u32[]{:S(2)}, u32[]{:S(2)}) async-start(f32[16,2,1,128,128]{4,3,2,1,0:T(8,128)} %broadcast_in_dim.29), calls=%async_computation.2 | async-start | bytes 4194304 | tf_op jit(solution)/shard_map/all_to_all | solution.py:22
  136.0 3.8 %copy-start.12 = (f32[2,128,128]{1,2,0:T(8,128)S(1)}, f32[2,128,128]{1,2,0:T(8,128)}, u32[]{:S(2)}) copy-start(f32[2,128,128]{1,2,0:T(8,128)} %reduce_window_sum.20) | copy-start | bytes 393220
  136.0 3.8 %copy-start.13 = (pred[2]{0:T(512)(128)(4,1)S(1)}, pred[2]{0:T(512)(128)(4,1)}, u32[]{:S(2)}) copy-start(pred[2]{0:T(512)(128)(4,1)} %constant.31.clone.1) | copy-start | bytes 10
  137.5 2.3 copy-start.6
  137.5 2.6 %copy-start.4 = (bf16[1024,128]{1,0:T(8,128)(2,1)S(1)}, bf16[1024,128]{1,0:T(8,128)(2,1)}, u32[]{:S(2)}) copy-start(bf16[1024,128]{1,0:T(8,128)(2,1)} %copy-done.3) | copy-start | bytes 786436
  138.9 2.5 %copy-start.2 = (bf16[1024,128]{1,0:T(8,128)(2,1)S(1)}, bf16[1024,128]{1,0:T(8,128)(2,1)}, u32[]{:S(2)}) copy-start(bf16[1024,128]{1,0:T(8,128)(2,1)} %copy-done.1) | copy-start | bytes 786436
  141.6 88.8 %copy-start.8 = (bf16[512,128]{1,0:T(8,128)(2,1)S(1)}, bf16[512,128]{1,0:T(8,128)(2,1)}, u32[]{:S(2)}) copy-start(bf16[512,128]{1,0:T(8,128)(2,1)} %param.19) | copy-start | bytes 393220
  141.6 89.1 %copy-start.9 = (bf16[512,128]{1,0:T(8,128)(2,1)S(1)}, bf16[512,128]{1,0:T(8,128)(2,1)}, u32[]{:S(2)}) copy-start(bf16[512,128]{1,0:T(8,128)(2,1)} %param.20) | copy-start | bytes 393220
  141.6 89.4 %copy-start.10 = (bf16[512,128]{1,0:T(8,128)(2,1)S(1)}, bf16[512,128]{1,0:T(8,128)(2,1)}, u32[]{:S(2)}) copy-start(bf16[512,128]{1,0:T(8,128)(2,1)} %param.17) | copy-start | bytes 393220
  142.8 88.6 %copy-start.11 = (bf16[512,128]{1,0:T(8,128)(2,1)S(1)}, bf16[512,128]{1,0:T(8,128)(2,1)}, u32[]{:S(2)}) copy-start(bf16[512,128]{1,0:T(8,128)(2,1)} %param.18) | copy-start | bytes 393220
where the time goes:
time: 235 us
  waiting for transfers between devices  147 us (63%)
  starting transfers between devices  57.7 us (25%)
  matrix products  11.1 us (5%)
  local copies, waits for them, and re-layouts  10 us (4%)
  other arithmetic  6.21 us (3%)
  between operations  2.44 us (1%)
    all_to_all x3, waiting for transfers between devices, sent_to_all(): lax.all_to_all(jnp.broadcast_to(value[None], (count, *value.shape)), axis...  128 us
    all_to_all x3, starting transfers between devices, sent_to_all(): lax.all_to_all(jnp.broadcast_to(value[None], (count, *value.shape)), axis...  37.7 us
    ppermute x4, starting transfers between devices, from_partner(): return lax.ppermute(value, axis, pairs)  20.1 us
    ppermute x4, waiting for transfers between devices, from_partner(): return lax.ppermute(value, axis, pairs)  19.5 us
  transfers between devices with their start and end apart: 7, of which 6 were waited for; matrix products, arithmetic and copies ran while one was open for 5% of the time, Pallas kernels for 0%

commit v1 on v0

v1 whole, which is shorter than its diff:
```python
import functools

import jax
import jax.numpy as jnp
from jax import lax
from jax.experimental import pallas as pl
from jax.experimental.pallas import tpu as pltpu
from jax.sharding import PartitionSpec as P

DH = 128
BLOCK = 512
EPSILON = 1e-06
F32 = jnp.float32
BF16 = jnp.bfloat16
MIB = 1 << 20

VM = pl.BlockSpec(memory_space=pltpu.VMEM)
SM = pl.BlockSpec(memory_space=pltpu.SMEM)


def dot(a, b, ca=1, cb=0):
    return lax.dot_general(a, b, (((ca,), (cb,)), ((), ())), preferred_element_type=F32)


def call(body, name, shapes, specs, flops=1000000, moved=1000000, limit=24):
    return pl.pallas_call(
        body,
        out_shape=[jax.ShapeDtypeStruct(s, d) for s, d in shapes],
        in_specs=specs,
        out_specs=[VM] * len(shapes),
        name=name,
        compiler_params=pltpu.CompilerParams(vmem_limit_bytes=limit * MIB),
        cost_estimate=pl.CostEstimate(flops=flops, bytes_accessed=moved, transcendentals=0),
    )


def chunked(ref, value, start, parts):
    rows = value.shape[0] // parts
    for part in range(parts):
        ref[part, start : start + rows, :] = value[part * rows : (part + 1) * rows]


def state_kernel(parts, branch_ref, tk_ref, tv_ref, bk_ref, bv_ref, out_ref):
    trunk = dot(tk_ref[...], tv_ref[...], 0, 0)
    branch = dot(bk_ref[...], bv_ref[...], 0, 0)
    rows = DH // parts
    chunked(out_ref, trunk, 0, parts)
    chunked(out_ref, branch, rows, parts)
    flag = jnp.full((8, DH), branch_ref[0], jnp.int32).astype(F32)
    for part in range(parts):
        out_ref[part, 2 * rows : 2 * rows + 8, :] = flag


def local_kernel(len_ref, q_ref, k_ref, v_ref, g_ref, gain_ref, qt_ref, km_ref, vm_ref, vt_ref, pt_ref, lt_ref, sgt_ref, first_ref):
    rows = q_ref.shape[0]
    keep = lax.broadcasted_iota(jnp.int32, (rows, DH), 0) < len_ref[0]
    km = jnp.where(keep, k_ref[...].astype(F32), 0.0).astype(BF16)
    vf = jnp.where(keep, v_ref[...].astype(F32), 0.0)
    vm = vf.astype(BF16)
    km_ref[...] = km
    vm_ref[...] = vm
    qt = q_ref[...].astype(F32).T.astype(BF16)
    vt = vf.T.astype(BF16)
    qt_ref[...] = qt
    vt_ref[...] = vt
    causal = lax.broadcasted_iota(jnp.int32, (BLOCK, BLOCK), 0) <= lax.broadcasted_iota(
        jnp.int32, (BLOCK, BLOCK), 1
    )
    for j in range(rows // BLOCK):
        s = slice(j * BLOCK, (j + 1) * BLOCK)
        pt = jnp.where(causal, dot(km[s], qt[:, s]), 0.0).astype(BF16)
        pt_ref[s, :] = pt
        lt_ref[:, s] = dot(vt[:, s], pt)
    for j in range(rows // BLOCK - 1):
        s = slice(j * BLOCK, (j + 1) * BLOCK)
        first_ref[j] = dot(km[s], vm[s], 0, 0)
    sgt_ref[...] = (g_ref[...].astype(F32) * gain_ref[...].astype(F32)).T


def half_sum_kernel(rows, in_ref, out_ref):
    total = in_ref[0, : 2 * rows, :]
    for part in range(1, in_ref.shape[0]):
        total = total + in_ref[part, : 2 * rows, :]
    out_ref[...] = total


def prefix_kernel(rows, members, own_ref, other_ref, flags_ref, out_ref):
    half = (lax.axis_index("leaf") // members).astype(F32)
    trunk = own_ref[:rows] + other_ref[:rows]
    mine = trunk + own_ref[rows:]
    others = trunk + other_ref[rows:]
    for part in range(members):
        flag = flags_ref[part, 2 * rows : 2 * rows + 1, :]
        out_ref[part] = jnp.where(flag == half, mine, others)


def raw_kernel(copies, len_ref, state_ref, first_ref, qt_ref, lt_ref, sgt_ref, states_ref, rawt_ref, out_ref):
    rows = qt_ref.shape[1]
    state = state_ref[...].reshape(DH, DH)
    earlier = None
    for j in range(rows // BLOCK):
        s = slice(j * BLOCK, (j + 1) * BLOCK)
        if j:
            earlier = first_ref[j - 1] if earlier is None else earlier + first_ref[j - 1]
        now = (state if earlier is None else state + earlier).astype(BF16)
        states_ref[j] = now
        keep = j * BLOCK + lax.broadcasted_iota(jnp.int32, (1, BLOCK), 1) < len_ref[0]
        raw = jnp.where(keep, dot(now, qt_ref[:, s], 0, 0) + lt_ref[:, s], 0.0)
        rawt_ref[:, s] = raw
        square = jnp.sum(raw * raw, axis=0, keepdims=True)
        inner = jnp.sum(raw * sgt_ref[:, s], axis=0, keepdims=True)
        for copy in range(copies):
            out_ref[copy, 0:1, s] = square
            out_ref[copy, 1:2, s] = inner


def spread_kernel(in_ref, out_ref):
    total = in_ref[0]
    for part in range(1, in_ref.shape[0]):
        total = total + in_ref[part]
    for copy in range(out_ref.shape[0]):
        out_ref[copy] = total


def grad_kernel(features, parts, len_ref, sums_ref, rawt_ref, sgt_ref, qt_ref, rgt_ref, norm_ref, later_ref, out_ref):
    rows = qt_ref.shape[1]
    total = sums_ref[0]
    for part in range(1, sums_ref.shape[0]):
        total = total + sums_ref[part]
    norm = lax.rsqrt(total[0:1] * (1.0 / features) + EPSILON)
    coef = norm * norm * norm * total[1:2] * (1.0 / features)
    norm_ref[...] = norm
    whole = None
    for j in reversed(range(rows // BLOCK)):
        s = slice(j * BLOCK, (j + 1) * BLOCK)
        keep = j * BLOCK + lax.broadcasted_iota(jnp.int32, (1, BLOCK), 1) < len_ref[0]
        rg = jnp.where(keep, norm[:, s] * sgt_ref[:, s] - rawt_ref[:, s] * coef[:, s], 0.0).astype(BF16)
        rgt_ref[:, s] = rg
        later_ref[j] = (jnp.zeros((DH, DH), F32) if whole is None else whole).astype(BF16)
        block = dot(qt_ref[:, s], rg, 1, 1)
        whole = block if whole is None else whole + block
    chunked(out_ref, whole, 0, parts)


def leaf_kernel(q_ref, km_ref, vm_ref, vt_ref, pt_ref, rgt_ref, states_ref, later_ref, rawt_ref, norm_ref, gain_ref, lo_ref, qg_ref, kg_ref, vg_ref):
    rows = q_ref.shape[0]
    lo_ref[...] = ((rawt_ref[...] * norm_ref[...]).T * gain_ref[...].astype(F32)).astype(BF16)
    first = lax.broadcasted_iota(jnp.int32, (BLOCK, BLOCK), 0)
    second = lax.broadcasted_iota(jnp.int32, (BLOCK, BLOCK), 1)
    for j in range(rows // BLOCK):
        s = slice(j * BLOCK, (j + 1) * BLOCK)
        rgt = rgt_ref[:, s]
        rg = rgt.astype(F32).T.astype(BF16)
        dp = jnp.where(second <= first, dot(rg, vt_ref[:, s]), 0.0).astype(BF16)
        qg_ref[s, :] = (dot(rg, states_ref[j], 1, 1) + dot(dp, km_ref[s, :])).astype(BF16)
        dpt = jnp.where(first <= second, dot(vm_ref[s, :], rgt), 0.0).astype(BF16)
        kg_ref[s, :] = (dot(dpt, q_ref[s, :]) + dot(vm_ref[s, :], later_ref[j], 1, 1)).astype(BF16)
        vg_ref[s, :] = (dot(pt_ref[s, :], rg) + dot(km_ref[s, :], later_ref[j])).astype(BF16)


def by_branch_kernel(rows, in_ref, flags_ref, out_ref):
    zero = one = None
    for part in range(in_ref.shape[0]):
        value = in_ref[part]
        first = flags_ref[part, 2 * rows : 2 * rows + 1, :] == 0.0
        a = jnp.where(first, value, 0.0)
        b = jnp.where(first, 0.0, value)
        zero = a if zero is None else zero + a
        one = b if one is None else one + b
    out_ref[:rows] = zero
    out_ref[rows:] = one


def total_kernel(rows, members, own_ref, other_ref, out_ref):
    zero = own_ref[:rows] + other_ref[:rows]
    one = own_ref[rows:] + other_ref[rows:]
    own = jnp.where(lax.axis_index("leaf") >= members, one, zero)
    both = zero + one
    for part in range(members):
        out_ref[part, :rows] = both
        out_ref[part, rows:] = own


def tree_kernel(rows, in_ref, tk_ref, tv_ref, bk_ref, bv_ref, tkg_ref, tvg_ref, bkg_ref, bvg_ref):
    for start, k_ref, v_ref, kg_ref, vg_ref in (
        (0, tk_ref, tv_ref, tkg_ref, tvg_ref),
        (rows, bk_ref, bv_ref, bkg_ref, bvg_ref),
    ):
        grad = in_ref[:, start : start + rows, :].reshape(DH, DH)
        high = grad.astype(BF16)
        rest = grad - high.astype(F32)
        middle = rest.astype(BF16)
        low = (rest - middle.astype(F32)).astype(BF16)
        keys, values = k_ref[...], v_ref[...]
        kg_ref[...] = (dot(values, high, 1, 1) + (dot(values, middle, 1, 1) + dot(values, low, 1, 1))).astype(BF16)
        vg_ref[...] = (dot(keys, high) + (dot(keys, middle) + dot(keys, low))).astype(BF16)


def shards(mesh_shape, leaf_query, leaf_keys, leaf_values, out_grad, leaf_len, branch_id, trunk_keys, trunk_values, branch_keys, branch_values, norm_gain):
    leaves, heads = mesh_shape
    rows = leaf_query.shape[0]
    tree_rows = trunk_keys.shape[0]
    blocks = rows // BLOCK
    members = leaves // 2
    part = DH // members
    halves = [[h * members + i for i in range(members)] for h in range(2)]
    near = 4
    far = heads // near
    near_groups = [[g * near + i for i in range(near)] for g in range(far)]
    far_groups = [[i + near * g for g in range(far)] for i in range(near)]
    across = [(i, i ^ members) for i in range(leaves)]
    gain = norm_gain.reshape(1, DH)

    def exchange(value, axis, groups):
        return lax.all_to_all(value, axis, 0, 0, tiled=True, axis_index_groups=groups)

    (sent,) = call(functools.partial(state_kernel, members), "state", [((members, 2 * part + 8, DH), F32)], [SM] + [VM] * 4)(
        branch_id, trunk_keys, trunk_values, branch_keys, branch_values
    )
    got = exchange(sent, "leaf", halves)
    qt, km, vm, vt, pt, lt, sgt, first = call(
        local_kernel,
        "local",
        [
            ((DH, rows), BF16),
            ((rows, DH), BF16),
            ((rows, DH), BF16),
            ((DH, rows), BF16),
            ((rows, BLOCK), BF16),
            ((DH, rows), F32),
            ((DH, rows), F32),
            ((blocks - 1, DH, DH), F32),
        ],
        [SM] + [VM] * 5,
        flops=4 * rows * BLOCK * DH,
        moved=6 * MIB,
    )(leaf_len, leaf_query, leaf_keys, leaf_values, out_grad, gain)
    (half,) = call(functools.partial(half_sum_kernel, part), "half", [((2 * part, DH), F32)], [VM])(got)
    other = lax.ppermute(half, "leaf", across)
    (chunk,) = call(functools.partial(prefix_kernel, part, members), "prefix", [((members, part, DH), F32)], [VM] * 3)(half, other, got)
    state = exchange(chunk, "leaf", halves)
    states, rawt, sums = call(
        functools.partial(raw_kernel, near),
        "raw",
        [((blocks, DH, DH), BF16), ((DH, rows), F32), ((near, 2, rows), F32)],
        [SM] + [VM] * 5,
    )(leaf_len, state, first, qt, lt, sgt)
    sums = exchange(sums, "head", near_groups)
    (sums,) = call(spread_kernel, "spread", [((far, 2, rows), F32)], [VM])(sums)
    sums = exchange(sums, "head", far_groups)
    rgt, norm, later, sent = call(
        functools.partial(grad_kernel, heads * DH, members),
        "grad",
        [((DH, rows), BF16), ((1, rows), F32), ((blocks, DH, DH), BF16), ((members, part, DH), F32)],
        [SM] + [VM] * 4,
    )(leaf_len, sums, rawt, sgt, qt)
    parts = exchange(sent, "leaf", halves)
    leaf = ((rows, DH), BF16)
    leaf_grads = call(
        leaf_kernel, "leaf", [leaf] * 4, [VM] * 11, flops=8 * rows * BLOCK * DH, moved=6 * MIB
    )(leaf_query, km, vm, vt, pt, rgt, states, later, rawt, norm, gain)
    (own,) = call(functools.partial(by_branch_kernel, part), "by_branch", [((2 * part, DH), F32)], [VM] * 2)(parts, got)
    other = lax.ppermute(own, "leaf", across)
    (sent,) = call(functools.partial(total_kernel, part, members), "total", [((members, 2 * part, DH), F32)], [VM] * 2)(own, other)
    grads = exchange(sent, "leaf", halves)
    tree = ((tree_rows, DH), BF16)
    tree_grads = call(functools.partial(tree_kernel, part), "tree", [tree] * 4, [VM] * 5)(
        grads, trunk_keys, trunk_values, branch_keys, branch_values
    )
    return (*leaf_grads, *tree_grads)


def solution(mesh):
    wide = P("leaf", "head")
    placed = (wide, wide, wide, wide, P("leaf"), P("leaf"), wide, wide, wide, wide, P("head"))
    return jax.shard_map(
        functools.partial(shards, (mesh.shape["leaf"], mesh.shape["head"])),
        mesh=mesh,
        in_specs=placed,
        out_specs=(wide,) * 8,
        check_vma=False,
    )
```

time: 235 us -> 121 us (0.51)
  the two profiles are of different devices: /device:TPU:193 before, /device:TPU:1 now
where the time goes in v1:
time: 121 us
  blocking collectives  72.9 us (60%)
  starting transfers between devices  20.6 us (17%)
  waiting for transfers between devices  9.92 us (8%)
  local copies, waits for them, and re-layouts  8.28 us (7%)
  Pallas kernels  6.99 us (6%)
  between operations  2.12 us (2%)
    all_to_all x4, blocking collectives, exchange(): lax.all_to_all(value, axis, 0, 0, tiled=True, axis_index_groups=groups)  72.9 us
    all_to_all x2, starting transfers between devices, exchange(): lax.all_to_all(value, axis, 0, 0, tiled=True, axis_index_groups=groups)  11.1 us
    unnamed x42, local copies, waits for them, and re-layouts  8.28 us
    ppermute x1, starting transfers between devices, shards(): other = lax.ppermute(own, 'leaf', across)  6.66 us
    ppermute x1, waiting for transfers between devices, shards(): other = lax.ppermute(half, 'leaf', across)  5.76 us
    ppermute x1, starting transfers between devices, shards(): other = lax.ppermute(half, 'leaf', across)  2.81 us
    pallas_call x1, Pallas kernels, shards(): call(leaf_kernel, 'leaf', [leaf] * 4, [VM] * 11, flops=8 * rows * BLOCK *...  2.63 us
  transfers between devices with their start and end apart: 4, of which 3 were waited for; matrix products, arithmetic and copies ran while one was open for 0% of the time, Pallas kernels for 3%

profile of v1, /device:TPU:1, one launch (start us, length us, event | category | flops | bytes accessed | tf_op | source)
XLA Modules:
  0.0 120.8 jit_solution(4879168403637235548)
XLA Ops:
  1.3 0.0 copy-start.1
  1.3 0.9 copy-done.1
  2.2 0.9 copy-done.3
  3.1 0.9 copy-done.5
  4.0 0.9 copy-done.7
  4.9 0.3 state.1
  5.2 0.0 copy-start.10
  5.2 22.7 %all_to_all.30.in_ref.flags_ref = f32[8,40,128]{2,1,0:T(8,128)S(1)} all-to-all(f32[8,40,128]{2,1,0:T(8,128)S(1)} %state.1), channel_id=1, replica_groups={{0,64,128,192,256,320,384,448},{512,576,640,704,768,832,896,960},{1,65,..., dimensions={0} | all-to-all | bytes 327680 | tf_op jit(solution)/shard_map/all_to_all | solution.py:215
  27.9 2.8 %collective-permute-start = (f32[32,128]{1,0:T(8,128)S(1)}, f32[32,128]{1,0:T(8,128)S(1)}, u32[]{:S(2)}, u32[]{:S(2)}) collective-permute-start(f32[32,128]{1,0:T(8,128)S(1)} %half.1.own_ref), channel_id=1, source_target_pairs={{0,512},{64,576},{128,640},{192,704},{256,768},{320,832},{384,896}... | collective-permute-start | bytes 49160 | tf_op jit(solution)/shard_map/ppermute | solution.py:239
  30.7 5.8 %collective-permute-done.other_ref = f32[32,128]{1,0:T(8,128)S(1)} collective-permute-done((f32[32,128]{1,0:T(8,128)S(1)}, f32[32,128]{1,0:T(8,128)S(1)}, u32[]{:S(2)}, u32[]{:S(2)}) %collective-permute-start) | collective-permute-done | bytes 16416 | tf_op jit(solution)/shard_map/ppermute | solution.py:239
  36.5 0.6 prefix.1
  37.1 5.5 %all-to-all-start.1 = ((f32[8,16,128]{2,1,0:T(8,128)}), f32[8,16,128]{2,1,0:T(8,128)S(1)}, u32[]{:S(2)}, u32[]{:S(2)}) async-start(f32[8,16,128]{2,1,0:T(8,128)} %prefix.1), calls=%async_computation.1 | async-start | bytes 131072 | tf_op jit(solution)/shard_map/all_to_all | solution.py:215
  43.3 0.0 copy-start.20
  43.3 0.0 copy-done.10
  43.3 0.0 copy-done
  43.3 0.0 copy-done.9
  43.3 0.6 copy-done.20
  43.9 0.9 copy-done.11
  44.9 0.9 local.1
  45.8 0.0 copy-start.12
  45.8 0.7 copy-done.12
  46.5 0.7 copy-done.14
  47.2 0.7 copy-done.16
  47.9 0.0 all-to-all-done.1.state_ref
  47.9 0.3 raw.1
  48.2 6.7 %all_to_all.31.in_ref = f32[4,2,1024]{2,1,0:T(2,128)S(1)} all-to-all(f32[4,2,1024]{2,1,0:T(2,128)S(1)} %get-tuple-element.39), channel_id=1, replica_groups={{0,1,2,3},{4,5,6,7},{8,9,10,11},{12,13,14,15},{16,17,18,19},{20,21,22,2..., dimensions={0} | all-to-all | bytes 65536 | tf_op jit(solution)/shard_map/all_to_all | solution.py:215
  54.9 30.6 %all_to_all.32.sums_ref = f32[16,2,1024]{2,1,0:T(2,128)S(1)} all-to-all(f32[16,2,1024]{2,1,0:T(2,128)S(1)} %spread.1), channel_id=1, replica_groups={{0,4,8,12,16,20,24,28,32,36,40,44,48,52,56,60},{1,5,9,13,17,21,25,29,33..., dimensions={0} | all-to-all | bytes 262144 | tf_op jit(solution)/shard_map/all_to_all | solution.py:215
  85.4 0.3 grad.1
  85.7 0.0 copy-start.18
  85.7 0.0 copy-start.17
  85.7 13.0 %all_to_all.33.in_ref = f32[8,16,128]{2,1,0:T(8,128)S(1)} all-to-all(f32[8,16,128]{2,1,0:T(8,128)S(1)} %get-tuple-element.49), channel_id=1, replica_groups={{0,64,128,192,256,320,384,448},{512,576,640,704,768,832,896,960},{1,65,..., dimensions={0} | all-to-all | bytes 131072 | tf_op jit(solution)/shard_map/all_to_all | solution.py:215
  98.7 0.0 copy-done.18
  98.7 0.0 copy-start.13
  98.8 6.7 %collective-permute-start.1 = (f32[32,128]{1,0:T(8,128)S(1)}, f32[32,128]{1,0:T(8,128)S(1)}, u32[]{:S(2)}, u32[]{:S(2)}) collective-permute-start(f32[32,128]{1,0:T(8,128)S(1)} %by_branch.1.own_ref), channel_id=1, source_target_pairs={{0,512},{64,576},{128,640},{192,704},{256,768},{320,832},{384,896}... | collective-permute-start | bytes 49160 | tf_op jit(solution)/shard_map/ppermute | solution.py:263
  105.4 1.9 %collective-permute-done.1.other_ref = f32[32,128]{1,0:T(8,128)S(1)} collective-permute-done((f32[32,128]{1,0:T(8,128)S(1)}, f32[32,128]{1,0:T(8,128)S(1)}, u32[]{:S(2)}, u32[]{:S(2)}) %collective-permute-start.1) | collective-permute-done | bytes 16416 | tf_op jit(solution)/shard_map/ppermute | solution.py:263
  107.4 0.7 total.1
  108.0 5.6 %all-to-all-start.5 = ((f32[8,32,128]{2,1,0:T(8,128)}), f32[8,32,128]{2,1,0:T(8,128)S(1)}, u32[]{:S(2)}, u32[]{:S(2)}) async-start(f32[8,32,128]{2,1,0:T(8,128)} %total.1), calls=%async_computation.5 | async-start | bytes 262144 | tf_op jit(solution)/shard_map/all_to_all | solution.py:215
  113.7 0.0 copy-done.17
  113.7 0.0 copy-done.15
  113.7 0.0 copy-done.13
  113.7 0.0 copy-start.19
  113.7 0.9 copy-done.19
  114.7 2.6 %leaf.1 = (bf16[1024,128]{1,0:T(8,128)(2,1)}, bf16[1024,128]{1,0:T(8,128)(2,1)}, bf16[1024,128]{1,0:T(8,128)(2,1)}, bf16[1024,128]{1,0:T(8,128)(2,1)}) custom-call(bf16[1024,128]{1,0:T(8,128)(2,1)S(1)} %copy-done, bf16[1024,128]{1,0:T(8,128)(2,1)S(1)} %copy-done.13, bf16[1024,128]{1,0:T(8,128)(2,1)S(1)} %copy-done.15, bf16[128,1024]{1,0:T(8,128)(2,1)S(1)} %copy-done.17, ...), custom_call_target="tpu_custom_call" | custom-call | flops 536870912 | bytes 6291456 | tf_op jit(solution)/shard_map/leaf/pallas_call | solution.py:259
  117.3 2.2 %all-to-all-done.5.in_ref = f32[8,32,128]{2,1,0:T(8,128)S(1)} async-done(((f32[8,32,128]{2,1,0:T(8,128)}), f32[8,32,128]{2,1,0:T(8,128)S(1)}, u32[]{:S(2)}, u32[]{:S(2)}) %all-to-all-start.5) | async-done | bytes 131104 | tf_op jit(solution)/shard_map/all_to_all | solution.py:215
  119.5 0.0 copy-done.2
  119.5 0.0 copy-done.4
  119.5 0.0 copy-done.6
  119.5 1.3 %tree.1 = (bf16[512,128]{1,0:T(8,128)(2,1)}, bf16[512,128]{1,0:T(8,128)(2,1)}, bf16[512,128]{1,0:T(8,128)(2,1)}, bf16[512,128]{1,0:T(8,128)(2,1)}) custom-call(f32[8,32,128]{2,1,0:T(8,128)S(1)} %all-to-all-done.5.in_ref, bf16[512,128]{1,0:T(8,128)(2,1)S(1)} %copy-done.2, bf16[512,128]{1,0:T(8,128)(2,1)S(1)} %copy-done.4, bf16[512,128]{1,0:T(8,128)(2,1)S(1)} %copy-done.6, ...), custom_call_target="tpu_custom_call" | custom-call | flops 1000000 | bytes 1000000 | tf_op jit(solution)/shard_map/tree/pallas_call | solution.py:267
  (17 shorter events, 0.1 us)
Async XLA Ops:
  1.3 0.9 copy-start.1
  2.2 0.9 copy-start.3
  3.1 0.9 copy-start.5
  4.0 0.9 copy-start.7
  5.2 38.1 %copy-start.10 = (bf16[1024,128]{1,0:T(8,128)(2,1)S(1)}, bf16[1024,128]{1,0:T(8,128)(2,1)}, u32[]{:S(2)}) copy-start(bf16[1024,128]{1,0:T(8,128)(2,1)} %v_ref.1) | copy-start | bytes 786436
  27.9 15.4 %copy-start = (bf16[1024,128]{1,0:T(8,128)(2,1)S(1)}, bf16[1024,128]{1,0:T(8,128)(2,1)}, u32[]{:S(2)}) copy-start(bf16[1024,128]{1,0:T(8,128)(2,1)} %q_ref.3) | copy-start | bytes 786436
  27.9 15.4 %copy-start.9 = (bf16[1024,128]{1,0:T(8,128)(2,1)S(1)}, bf16[1024,128]{1,0:T(8,128)(2,1)}, u32[]{:S(2)}) copy-start(bf16[1024,128]{1,0:T(8,128)(2,1)} %k_ref.1) | copy-start | bytes 786436
  27.9 8.6 %collective-permute-start = (f32[32,128]{1,0:T(8,128)S(1)}, f32[32,128]{1,0:T(8,128)S(1)}, u32[]{:S(2)}, u32[]{:S(2)}) collective-permute-start(f32[32,128]{1,0:T(8,128)S(1)} %half.1.own_ref), channel_id=1, source_target_pairs={{0,512},{64,576},{128,640},{192,704},{256,768},{320,832},{384,896}... | collective-permute-start | bytes 49160 | tf_op jit(solution)/shard_map/ppermute | solution.py:239
  37.1 10.8 %all-to-all-start.1 = ((f32[8,16,128]{2,1,0:T(8,128)}), f32[8,16,128]{2,1,0:T(8,128)S(1)}, u32[]{:S(2)}, u32[]{:S(2)}) async-start(f32[8,16,128]{2,1,0:T(8,128)} %prefix.1), calls=%async_computation.1 | async-start | bytes 131072 | tf_op jit(solution)/shard_map/all_to_all | solution.py:215
  43.3 0.7 copy-start.20
  43.9 0.9 copy-start.11
  45.8 0.7 copy-start.12
  46.5 0.7 copy-start.14
  47.2 0.7 copy-start.16
  85.7 13.0 %copy-start.18 = (bf16[128,1024]{1,0:T(8,128)(2,1)}, bf16[128,1024]{1,0:T(8,128)(2,1)S(1)}, u32[]{:S(2)}) copy-start(bf16[128,1024]{1,0:T(8,128)(2,1)S(1)} %get-tuple-element.41.rgt_ref) | copy-start | bytes 786436
  85.7 28.0 %copy-start.17 = (bf16[128,1024]{1,0:T(8,128)(2,1)S(1)}, bf16[128,1024]{1,0:T(8,128)(2,1)}, u32[]{:S(2)}) copy-start(bf16[128,1024]{1,0:T(8,128)(2,1)} %copy-done.16) | copy-start | bytes 786436
  98.7 15.0 %copy-start.15 = (bf16[1024,128]{1,0:T(8,128)(2,1)S(1)}, bf16[1024,128]{1,0:T(8,128)(2,1)}, u32[]{:S(2)}) copy-start(bf16[1024,128]{1,0:T(8,128)(2,1)} %copy-done.14) | copy-start | bytes 786436
  98.7 14.9 %copy-start.13 = (bf16[1024,128]{1,0:T(8,128)(2,1)S(1)}, bf16[1024,128]{1,0:T(8,128)(2,1)}, u32[]{:S(2)}) copy-start(bf16[1024,128]{1,0:T(8,128)(2,1)} %copy-done.12) | copy-start | bytes 786436
  98.8 8.6 %collective-permute-start.1 = (f32[32,128]{1,0:T(8,128)S(1)}, f32[32,128]{1,0:T(8,128)S(1)}, u32[]{:S(2)}, u32[]{:S(2)}) collective-permute-start(f32[32,128]{1,0:T(8,128)S(1)} %by_branch.1.own_ref), channel_id=1, source_target_pairs={{0,512},{64,576},{128,640},{192,704},{256,768},{320,832},{384,896}... | collective-permute-start | bytes 49160 | tf_op jit(solution)/shard_map/ppermute | solution.py:263
  108.0 11.5 %all-to-all-start.5 = ((f32[8,32,128]{2,1,0:T(8,128)}), f32[8,32,128]{2,1,0:T(8,128)S(1)}, u32[]{:S(2)}, u32[]{:S(2)}) async-start(f32[8,32,128]{2,1,0:T(8,128)} %total.1), calls=%async_computation.5 | async-start | bytes 262144 | tf_op jit(solution)/shard_map/all_to_all | solution.py:215
  113.7 1.0 copy-start.19
  114.7 4.9 %copy-start.2 = (bf16[512,128]{1,0:T(8,128)(2,1)S(1)}, bf16[512,128]{1,0:T(8,128)(2,1)}, u32[]{:S(2)}) copy-start(bf16[512,128]{1,0:T(8,128)(2,1)} %tk_ref.3) | copy-start | bytes 393220
  114.7 4.9 %copy-start.4 = (bf16[512,128]{1,0:T(8,128)(2,1)S(1)}, bf16[512,128]{1,0:T(8,128)(2,1)}, u32[]{:S(2)}) copy-start(bf16[512,128]{1,0:T(8,128)(2,1)} %tv_ref.3) | copy-start | bytes 393220
  114.7 4.9 %copy-start.6 = (bf16[512,128]{1,0:T(8,128)(2,1)S(1)}, bf16[512,128]{1,0:T(8,128)(2,1)}, u32[]{:S(2)}) copy-start(bf16[512,128]{1,0:T(8,128)(2,1)} %bk_ref.3) | copy-start | bytes 393220
  114.7 4.9 %copy-start.8 = (bf16[512,128]{1,0:T(8,128)(2,1)S(1)}, bf16[512,128]{1,0:T(8,128)(2,1)}, u32[]{:S(2)}) copy-start(bf16[512,128]{1,0:T(8,128)(2,1)} %bv_ref.3) | copy-start | bytes 393220

commit v2 on v1

--- a/solution.py
+++ b/solution.py
@@ -16,18 +16,21 @@
 
 VM = pl.BlockSpec(memory_space=pltpu.VMEM)
 SM = pl.BlockSpec(memory_space=pltpu.SMEM)
+HB = pl.BlockSpec(memory_space=pltpu.MemorySpace.HBM)
+ANY = pl.BlockSpec(memory_space=pl.ANY)
 
 
 def dot(a, b, ca=1, cb=0):
     return lax.dot_general(a, b, (((ca,), (cb,)), ((), ())), preferred_element_type=F32)
 
 
-def call(body, name, shapes, specs, flops=1000000, moved=1000000, limit=24):
+def call(body, name, shapes, specs, flops=1000000, moved=1000000, limit=24, out=None, scratch=()):
     return pl.pallas_call(
         body,
         out_shape=[jax.ShapeDtypeStruct(s, d) for s, d in shapes],
         in_specs=specs,
-        out_specs=[VM] * len(shapes),
+        out_specs=out or [VM] * len(shapes),
+        scratch_shapes=list(scratch),
         name=name,
         compiler_params=pltpu.CompilerParams(vmem_limit_bytes=limit * MIB),
         cost_estimate=pl.CostEstimate(flops=flops, bytes_accessed=moved, transcendentals=0),
@@ -40,18 +43,28 @@
         ref[part, start : start + rows, :] = value[part * rows : (part + 1) * rows]
 
 
-def state_kernel(parts, branch_ref, tk_ref, tv_ref, bk_ref, bv_ref, out_ref):
-    trunk = dot(tk_ref[...], tv_ref[...], 0, 0)
-    branch = dot(bk_ref[...], bv_ref[...], 0, 0)
+def state_kernel(parts, len_ref, branch_ref, tk_hbm, tv_hbm, bk_hbm, bv_hbm, out_ref, tk_ref, tv_ref, bk_ref, bv_ref, sems):
+    copies = [
+        pltpu.make_async_copy(source, target, sems.at[i])
+        for i, (source, target) in enumerate(
+            ((tk_hbm, tk_ref), (tv_hbm, tv_ref), (bk_hbm, bk_ref), (bv_hbm, bv_ref))
+        )
+    ]
+    for copy in copies:
+        copy.start()
     rows = DH // parts
-    chunked(out_ref, trunk, 0, parts)
-    chunked(out_ref, branch, rows, parts)
+    copies[0].wait()
+    copies[1].wait()
+    chunked(out_ref, dot(tk_ref[...], tv_ref[...], 0, 0), 0, parts)
+    copies[2].wait()
+    copies[3].wait()
+    chunked(out_ref, dot(bk_ref[...], bv_ref[...], 0, 0), rows, parts)
     flag = jnp.full((8, DH), branch_ref[0], jnp.int32).astype(F32)
     for part in range(parts):
         out_ref[part, 2 * rows : 2 * rows + 8, :] = flag
 
 
-def local_kernel(len_ref, q_ref, k_ref, v_ref, g_ref, gain_ref, qt_ref, km_ref, vm_ref, vt_ref, pt_ref, lt_ref, sgt_ref, first_ref):
+def local_kernel(len_ref, q_ref, k_ref, v_ref, g_ref, gain_ref, after_ref, qt_ref, km_ref, vm_ref, vt_ref, pt_ref, lt_ref, sgt_ref, first_ref):
     rows = q_ref.shape[0]
     keep = lax.broadcasted_iota(jnp.int32, (rows, DH), 0) < len_ref[0]
     km = jnp.where(keep, k_ref[...].astype(F32), 0.0).astype(BF16)
@@ -84,7 +97,7 @@
     out_ref[...] = total
 
 
-def prefix_kernel(rows, members, own_ref, other_ref, flags_ref, out_ref):
+def prefix_kernel(rows, members, own_ref, other_ref, flags_ref, after_ref, out_ref):
     half = (lax.axis_index("leaf") // members).astype(F32)
     trunk = own_ref[:rows] + other_ref[:rows]
     mine = trunk + own_ref[rows:]
@@ -142,7 +155,8 @@
     chunked(out_ref, whole, 0, parts)
 
 
-def leaf_kernel(q_ref, km_ref, vm_ref, vt_ref, pt_ref, rgt_ref, states_ref, later_ref, rawt_ref, norm_ref, gain_ref, lo_ref, qg_ref, kg_ref, vg_ref):
+def leaf_kernel(q_ref, km_ref, vm_ref, vt_ref, pt_ref, rgt_ref, states_ref, later_ref, rawt_ref, norm_ref, gain_ref, after_ref, lo_ref, qg_ref, kg_ref, vg_ref, done_ref):
+    done_ref[...] = jnp.zeros_like(done_ref)
     rows = q_ref.shape[0]
     lo_ref[...] = ((rawt_ref[...] * norm_ref[...]).T * gain_ref[...].astype(F32)).astype(BF16)
     first = lax.broadcasted_iota(jnp.int32, (BLOCK, BLOCK), 0)
@@ -171,7 +185,7 @@
     out_ref[rows:] = one
 
 
-def total_kernel(rows, members, own_ref, other_ref, out_ref):
+def total_kernel(rows, members, own_ref, other_ref, after_ref, out_ref):
     zero = own_ref[:rows] + other_ref[:rows]
     one = own_ref[rows:] + other_ref[rows:]
     own = jnp.where(lax.axis_index("leaf") >= members, one, zero)
@@ -181,10 +195,15 @@
         out_ref[part, rows:] = own
 
 
-def tree_kernel(rows, in_ref, tk_ref, tv_ref, bk_ref, bv_ref, tkg_ref, tvg_ref, bkg_ref, bvg_ref):
-    for start, k_ref, v_ref, kg_ref, vg_ref in (
-        (0, tk_ref, tv_ref, tkg_ref, tvg_ref),
-        (rows, bk_ref, bv_ref, bkg_ref, bvg_ref),
+def tree_kernel(rows, in_ref, tk_ref, tv_ref, bk_ref, bv_ref, tkg_hbm, tvg_hbm, bkg_hbm, bvg_hbm, tkg_ref, tvg_ref, bkg_ref, bvg_ref, sems):
+    copies = [
+        pltpu.make_async_copy(source, target, sems.at[i])
+        for i, (source, target) in enumerate(
+            ((tkg_ref, tkg_hbm), (tvg_ref, tvg_hbm), (bkg_ref, bkg_hbm), (bvg_ref, bvg_hbm))
+        )
+    ]
+    for i, (start, k_ref, v_ref, kg_ref, vg_ref) in enumerate(
+        ((0, tk_ref, tv_ref, tkg_ref, tvg_ref), (rows, bk_ref, bv_ref, bkg_ref, bvg_ref))
     ):
         grad = in_ref[:, start : start + rows, :].reshape(DH, DH)
         high = grad.astype(BF16)
@@ -193,7 +212,11 @@
         low = (rest - middle.astype(F32)).astype(BF16)
         keys, values = k_ref[...], v_ref[...]
         kg_ref[...] = (dot(values, high, 1, 1) + (dot(values, middle, 1, 1) + dot(values, low, 1, 1))).astype(BF16)
+        copies[2 * i].start()
         vg_ref[...] = (dot(keys, high) + (dot(keys, middle) + dot(keys, low))).astype(BF16)
+        copies[2 * i + 1].start()
+    for copy in copies:
+        copy.wait()
 
 
 def shards(mesh_shape, leaf_query, leaf_keys, leaf_values, out_grad, leaf_len, branch_id, trunk_keys, trunk_values, branch_keys, branch_values, norm_gain):
@@ -214,10 +237,18 @@
     def exchange(value, axis, groups):
         return lax.all_to_all(value, axis, 0, 0, tiled=True, axis_index_groups=groups)
 
-    (sent,) = call(functools.partial(state_kernel, members), "state", [((members, 2 * part + 8, DH), F32)], [SM] + [VM] * 4)(
-        branch_id, trunk_keys, trunk_values, branch_keys, branch_values
-    )
+    held = pltpu.VMEM((tree_rows, DH), BF16)
+    stay = functools.partial(pltpu.with_memory_space_constraint, memory_space=pltpu.MemorySpace.HBM)
+    (sent,) = call(
+        functools.partial(state_kernel, members),
+        "state",
+        [((members, 2 * part + 8, DH), F32)],
+        [SM] * 2 + [HB] * 4,
+        scratch=[held] * 4 + [pltpu.SemaphoreType.DMA((4,))],
+    )(leaf_len, branch_id, *map(stay, (trunk_keys, trunk_values, branch_keys, branch_values)))
     got = exchange(sent, "leaf", halves)
+    (half,) = call(functools.partial(half_sum_kernel, part), "half", [((2 * part, DH), F32)], [VM])(got)
+    other = lax.ppermute(half, "leaf", across)
     qt, km, vm, vt, pt, lt, sgt, first = call(
         local_kernel,
         "local",
@@ -231,13 +262,13 @@
             ((DH, rows), F32),
             ((blocks - 1, DH, DH), F32),
         ],
-        [SM] + [VM] * 5,
+        [SM] + [VM] * 5 + [ANY],
         flops=4 * rows * BLOCK * DH,
         moved=6 * MIB,
-    )(leaf_len, leaf_query, leaf_keys, leaf_values, out_grad, gain)
-    (half,) = call(functools.partial(half_sum_kernel, part), "half", [((2 * part, DH), F32)], [VM])(got)
-    other = lax.ppermute(half, "leaf", across)
-    (chunk,) = call(functools.partial(prefix_kernel, part, members), "prefix", [((members, part, DH), F32)], [VM] * 3)(half, other, got)
+    )(leaf_len, leaf_query, leaf_keys, leaf_values, out_grad, gain, half)
+    (chunk,) = call(
+        functools.partial(prefix_kernel, part, members), "prefix", [((members, part, DH), F32)], [VM] * 3 + [ANY]
+    )(half, other, got, first)
     state = exchange(chunk, "leaf", halves)
     states, rawt, sums = call(
         functools.partial(raw_kernel, near),
@@ -256,17 +287,24 @@
     )(leaf_len, sums, rawt, sgt, qt)
     parts = exchange(sent, "leaf", halves)
     leaf = ((rows, DH), BF16)
-    leaf_grads = call(
-        leaf_kernel, "leaf", [leaf] * 4, [VM] * 11, flops=8 * rows * BLOCK * DH, moved=6 * MIB
-    )(leaf_query, km, vm, vt, pt, rgt, states, later, rawt, norm, gain)
     (own,) = call(functools.partial(by_branch_kernel, part), "by_branch", [((2 * part, DH), F32)], [VM] * 2)(parts, got)
     other = lax.ppermute(own, "leaf", across)
-    (sent,) = call(functools.partial(total_kernel, part, members), "total", [((members, 2 * part, DH), F32)], [VM] * 2)(own, other)
+    *leaf_grads, done = call(
+        leaf_kernel, "leaf", [leaf] * 4 + [((8, DH), F32)], [VM] * 11 + [ANY], flops=8 * rows * BLOCK * DH, moved=6 * MIB
+    )(leaf_query, km, vm, vt, pt, rgt, states, later, rawt, norm, gain, own)
+    (sent,) = call(
+        functools.partial(total_kernel, part, members), "total", [((members, 2 * part, DH), F32)], [VM] * 2 + [ANY]
+    )(own, other, done)
     grads = exchange(sent, "leaf", halves)
     tree = ((tree_rows, DH), BF16)
-    tree_grads = call(functools.partial(tree_kernel, part), "tree", [tree] * 4, [VM] * 5)(
-        grads, trunk_keys, trunk_values, branch_keys, branch_values
-    )
+    tree_grads = call(
+        functools.partial(tree_kernel, part),
+        "tree",
+        [tree] * 4,
+        [VM] * 5,
+        out=[HB] * 4,
+        scratch=[held] * 4 + [pltpu.SemaphoreType.DMA((4,))],
+    )(grads, trunk_keys, trunk_values, branch_keys, branch_values)
     return (*leaf_grads, *tree_grads)
 
 

time: 121 us -> 116 us (0.959)
  blocking collectives: 72.9 us -> 92.8 us
  starting transfers between devices: 20.6 us -> 7.64 us
  local copies, waits for them, and re-layouts: 8.28 us -> 0.05 us
  waiting for transfers between devices: 9.92 us -> 5.65 us
    all_to_all x4 -> x6, blocking collectives: 72.9 us -> 92.8 us  [exchange(): lax.all_to_all(value, axis, 0, 0, tiled=True, axis_index_groups=groups)]
    all_to_all x2 -> x0, starting transfers between devices: 11.1 us -> none  [exchange(): lax.all_to_all(value, axis, 0, 0, tiled=True, axis_index_groups=groups)]
    unnamed x42 -> x18, local copies, waits for them, and re-layouts: 8.28 us -> 0.05 us
    all_to_all x2 -> x0, waiting for transfers between devices: 2.21 us -> none  [exchange(): lax.all_to_all(value, axis, 0, 0, tiled=True, axis_index_groups=groups)]
    ppermute x1, starting transfers between devices: 6.66 us -> 4.96 us  [shards(): other = lax.ppermute(own, 'leaf', across)]
    pallas_call x1, Pallas kernels: 0.27 us -> 1.54 us  [shards(): call(functools.partial(state_kernel, members), 'state', [((members, 2 * p...]
  transfers between devices with their start and end apart: 4 -> 2, of which waited for: 3 -> 2; matrix products, arithmetic and copies ran while one was open for 0% -> 0% of each run, Pallas kernels for 3% -> 3%
where the time goes in v2:
time: 116 us; the launch traced here: 115 us
  blocking collectives  92.8 us (80%)
  starting transfers between devices  7.64 us (7%)
  Pallas kernels  7.04 us (6%)
  waiting for transfers between devices  5.65 us (5%)
  between operations  2.11 us (2%)
    all_to_all x6, blocking collectives, exchange(): lax.all_to_all(value, axis, 0, 0, tiled=True, axis_index_groups=groups)  92.8 us
    ppermute x1, starting transfers between devices, shards(): other = lax.ppermute(own, 'leaf', across)  4.96 us
    ppermute x1, waiting for transfers between devices, shards(): other = lax.ppermute(half, 'leaf', across)  4.8 us
    ppermute x1, starting transfers between devices, shards(): other = lax.ppermute(half, 'leaf', across)  2.68 us
    pallas_call x1, Pallas kernels, shards(): call(leaf_kernel, 'leaf', [leaf] * 4 + [((8, DH), F32)], [VM] * 11 + [ANY...  2.65 us
  transfers between devices with their start and end apart: 2, of which 2 were waited for; matrix products, arithmetic and copies ran while one was open for 0% of the time, Pallas kernels for 3%

profile of v2, /device:TPU:1, one launch (start us, length us, event | category | flops | bytes accessed | tf_op | source)
XLA Modules:
  0.0 115.3 jit_solution(16552783718160387276)
XLA Ops:
  1.9 0.0 copy-start.5
  1.9 0.0 copy-start.6
  1.9 0.0 copy-start.7
  2.0 1.5 %state.1 = f32[8,40,128]{2,1,0:T(8,128)S(1)} custom-call(s32[1]{0:T(128)S(6)} %copy.19.len_ref, s32[1]{0:T(128)S(6)} %copy.20.branch_ref, bf16[512,128]{1,0:T(8,128)(2,1)} %tk_ref.1, bf16[512,128]{1,0:T(8,128)(2,1)} %tv_ref.1, bf16[512,128]{1,0:T(8,128)(2,1)} %bk_ref.1, bf16[512,128]{1,0:T(8,128)(2,1)} %bv_ref.1), custom_call_target="tpu_custom_call" | custom-call | flops 1000000 | bytes 1000000 | tf_op jit(solution)/shard_map/state/pallas_call | solution.py:242
  3.5 0.0 copy-start
  3.5 22.7 %all_to_all.30.in_ref.flags_ref = f32[8,40,128]{2,1,0:T(8,128)S(1)} all-to-all(f32[8,40,128]{2,1,0:T(8,128)S(1)} %state.1), channel_id=1, replica_groups={{0,64,128,192,256,320,384,448},{512,576,640,704,768,832,896,960},{1,65,..., dimensions={0} | all-to-all | bytes 327680 | tf_op jit(solution)/shard_map/all_to_all | solution.py:238
  26.2 0.0 copy-start.8
  26.2 2.7 %collective-permute-start = (f32[32,128]{1,0:T(8,128)S(1)}, f32[32,128]{1,0:T(8,128)S(1)}, u32[]{:S(2)}, u32[]{:S(2)}) collective-permute-start(f32[32,128]{1,0:T(8,128)S(1)} %half.1.after_ref.own_ref), channel_id=1, source_target_pairs={{0,512},{64,576},{128,640},{192,704},{256,768},{320,832},{384,896}... | collective-permute-start | bytes 49160 | tf_op jit(solution)/shard_map/ppermute | solution.py:251
  28.9 0.0 copy-done.5
  28.9 0.0 copy-done.6
  28.9 0.0 copy-done.7
  28.9 0.0 copy-done
  29.0 0.0 copy-done.8
  29.0 0.9 local.1
  29.9 4.8 %collective-permute-done.other_ref = f32[32,128]{1,0:T(8,128)S(1)} collective-permute-done((f32[32,128]{1,0:T(8,128)S(1)}, f32[32,128]{1,0:T(8,128)S(1)}, u32[]{:S(2)}, u32[]{:S(2)}) %collective-permute-start) | collective-permute-done | bytes 16416 | tf_op jit(solution)/shard_map/ppermute | solution.py:251
  34.7 10.0 %all_to_all.31.state_ref = f32[8,16,128]{2,1,0:T(8,128)S(1)} all-to-all(f32[8,16,128]{2,1,0:T(8,128)S(1)} %prefix.1), channel_id=1, replica_groups={{0,64,128,192,256,320,384,448},{512,576,640,704,768,832,896,960},{1,65,..., dimensions={0} | all-to-all | bytes 131072 | tf_op jit(solution)/shard_map/all_to_all | solution.py:238
  44.7 0.3 raw.1
  45.1 6.7 %all_to_all.32.in_ref = f32[4,2,1024]{2,1,0:T(2,128)S(1)} all-to-all(f32[4,2,1024]{2,1,0:T(2,128)S(1)} %get-tuple-element.40), channel_id=1, replica_groups={{0,1,2,3},{4,5,6,7},{8,9,10,11},{12,13,14,15},{16,17,18,19},{20,21,22,2..., dimensions={0} | all-to-all | bytes 65536 | tf_op jit(solution)/shard_map/all_to_all | solution.py:238
  51.7 30.6 %all_to_all.33.sums_ref = f32[16,2,1024]{2,1,0:T(2,128)S(1)} all-to-all(f32[16,2,1024]{2,1,0:T(2,128)S(1)} %spread.1), channel_id=1, replica_groups={{0,4,8,12,16,20,24,28,32,36,40,44,48,52,56,60},{1,5,9,13,17,21,25,29,33..., dimensions={0} | all-to-all | bytes 262144 | tf_op jit(solution)/shard_map/all_to_all | solution.py:238
  82.3 0.3 grad.1
  82.6 12.1 %all_to_all.34.in_ref = f32[8,16,128]{2,1,0:T(8,128)S(1)} all-to-all(f32[8,16,128]{2,1,0:T(8,128)S(1)} %get-tuple-element.46), channel_id=1, replica_groups={{0,64,128,192,256,320,384,448},{512,576,640,704,768,832,896,960},{1,65,..., dimensions={0} | all-to-all | bytes 131072 | tf_op jit(solution)/shard_map/all_to_all | solution.py:238
  94.8 5.0 %collective-permute-start.1 = (f32[32,128]{1,0:T(8,128)S(1)}, f32[32,128]{1,0:T(8,128)S(1)}, u32[]{:S(2)}, u32[]{:S(2)}) collective-permute-start(f32[32,128]{1,0:T(8,128)S(1)} %by_branch.1.after_ref.own_ref), channel_id=1, source_target_pairs={{0,512},{64,576},{128,640},{192,704},{256,768},{320,832},{384,896}... | collective-permute-start | bytes 49160 | tf_op jit(solution)/shard_map/ppermute | solution.py:291
  99.7 0.0 copy-start.4
  99.8 2.6 %leaf.1 = (bf16[1024,128]{1,0:T(8,128)(2,1)}, bf16[1024,128]{1,0:T(8,128)(2,1)}, bf16[1024,128]{1,0:T(8,128)(2,1)}, bf16[1024,128]{1,0:T(8,128)(2,1)}, f32[8,128]{1,0:T(8,128)S(1)}) custom-call(bf16[1024,128]{1,0:T(8,128)(2,1)S(1)} %copy-done, bf16[1024,128]{1,0:T(8,128)(2,1)S(1)} %get-tuple-element.32.km_ref, ...), custom_call_target="tpu_custom_call" | custom-call | flops 536870912 | bytes 6291456 | tf_op jit(solution)/shard_map/leaf/pallas_call | solution.py:292
  102.4 0.8 collective-permute-done.1.other_ref
  103.3 0.0 copy-start.3
  103.3 0.0 copy-start.1
  103.3 0.0 copy-start.2
  103.3 10.7 %all_to_all.35.in_ref = f32[8,32,128]{2,1,0:T(8,128)S(1)} all-to-all(f32[8,32,128]{2,1,0:T(8,128)S(1)} %total.1), channel_id=1, replica_groups={{0,64,128,192,256,320,384,448},{512,576,640,704,768,832,896,960},{1,65,..., dimensions={0} | all-to-all | bytes 262144 | tf_op jit(solution)/shard_map/all_to_all | solution.py:238
  114.0 0.0 copy-done.4
  114.0 0.0 copy-done.3
  114.0 0.0 copy-done.1
  114.0 0.0 copy-done.2
  114.0 1.3 %tree.1 = (bf16[512,128]{1,0:T(8,128)(2,1)}, bf16[512,128]{1,0:T(8,128)(2,1)}, bf16[512,128]{1,0:T(8,128)(2,1)}, bf16[512,128]{1,0:T(8,128)(2,1)}) custom-call(f32[8,32,128]{2,1,0:T(8,128)S(1)} %all_to_all.35.in_ref, bf16[512,128]{1,0:T(8,128)(2,1)S(1)} %copy-done.1, bf16[512,128]{1,0:T(8,128)(2,1)S(1)} %copy-done.2, bf16[512,128]{1,0:T(8,128)(2,1)S(1)} %copy-done.3, ...), custom_call_target="tpu_custom_call" | custom-call | flops 1000000 | bytes 1000000 | tf_op jit(solution)/shard_map/tree/pallas_call | solution.py:300
  (5 shorter events, 0.1 us)
Async XLA Ops:
  1.9 27.0 %copy-start.5 = (bf16[1024,128]{1,0:T(8,128)(2,1)S(1)}, bf16[1024,128]{1,0:T(8,128)(2,1)}, u32[]{:S(2)}) copy-start(bf16[1024,128]{1,0:T(8,128)(2,1)} %k_ref.1) | copy-start | bytes 786436
  1.9 27.0 %copy-start.6 = (bf16[1024,128]{1,0:T(8,128)(2,1)S(1)}, bf16[1024,128]{1,0:T(8,128)(2,1)}, u32[]{:S(2)}) copy-start(bf16[1024,128]{1,0:T(8,128)(2,1)} %v_ref.1) | copy-start | bytes 786436
  1.9 27.0 %copy-start.7 = (bf16[1024,128]{1,0:T(8,128)(2,1)S(1)}, bf16[1024,128]{1,0:T(8,128)(2,1)}, u32[]{:S(2)}) copy-start(bf16[1024,128]{1,0:T(8,128)(2,1)} %g_ref.1) | copy-start | bytes 786436
  3.5 25.4 %copy-start = (bf16[1024,128]{1,0:T(8,128)(2,1)S(1)}, bf16[1024,128]{1,0:T(8,128)(2,1)}, u32[]{:S(2)}) copy-start(bf16[1024,128]{1,0:T(8,128)(2,1)} %q_ref.3) | copy-start | bytes 786436
  26.2 2.7 %copy-start.8 = (bf16[128]{0:T(256)(128)(2,1)S(1)}, bf16[128]{0:T(256)(128)(2,1)}, u32[]{:S(2)}) copy-start(bf16[128]{0:T(256)(128)(2,1)} %param.21) | copy-start | bytes 772
  26.2 8.5 %collective-permute-start = (f32[32,128]{1,0:T(8,128)S(1)}, f32[32,128]{1,0:T(8,128)S(1)}, u32[]{:S(2)}, u32[]{:S(2)}) collective-permute-start(f32[32,128]{1,0:T(8,128)S(1)} %half.1.after_ref.own_ref), channel_id=1, source_target_pairs={{0,512},{64,576},{128,640},{192,704},{256,768},{320,832},{384,896}... | collective-permute-start | bytes 49160 | tf_op jit(solution)/shard_map/ppermute | solution.py:251
  94.8 8.5 %collective-permute-start.1 = (f32[32,128]{1,0:T(8,128)S(1)}, f32[32,128]{1,0:T(8,128)S(1)}, u32[]{:S(2)}, u32[]{:S(2)}) collective-permute-start(f32[32,128]{1,0:T(8,128)S(1)} %by_branch.1.after_ref.own_ref), channel_id=1, source_target_pairs={{0,512},{64,576},{128,640},{192,704},{256,768},{320,832},{384,896}... | collective-permute-start | bytes 49160 | tf_op jit(solution)/shard_map/ppermute | solution.py:291
  99.7 14.2 %copy-start.4 = (bf16[512,128]{1,0:T(8,128)(2,1)S(1)}, bf16[512,128]{1,0:T(8,128)(2,1)}, u32[]{:S(2)}) copy-start(bf16[512,128]{1,0:T(8,128)(2,1)} %bv_ref.1) | copy-start | bytes 393220
  103.3 10.7 %copy-start.3 = (bf16[512,128]{1,0:T(8,128)(2,1)S(1)}, bf16[512,128]{1,0:T(8,128)(2,1)}, u32[]{:S(2)}) copy-start(bf16[512,128]{1,0:T(8,128)(2,1)} %bk_ref.1) | copy-start | bytes 393220
  103.3 10.7 %copy-start.1 = (bf16[512,128]{1,0:T(8,128)(2,1)S(1)}, bf16[512,128]{1,0:T(8,128)(2,1)}, u32[]{:S(2)}) copy-start(bf16[512,128]{1,0:T(8,128)(2,1)} %tk_ref.1) | copy-start | bytes 393220
  103.3 10.7 %copy-start.2 = (bf16[512,128]{1,0:T(8,128)(2,1)S(1)}, bf16[512,128]{1,0:T(8,128)(2,1)}, u32[]{:S(2)}) copy-start(bf16[512,128]{1,0:T(8,128)(2,1)} %tv_ref.1) | copy-start | bytes 393220

commit v3 on v2

--- a/solution.py
+++ b/solution.py
@@ -43,7 +43,7 @@
         ref[part, start : start + rows, :] = value[part * rows : (part + 1) * rows]
 
 
-def state_kernel(parts, len_ref, branch_ref, tk_hbm, tv_hbm, bk_hbm, bv_hbm, out_ref, tk_ref, tv_ref, bk_ref, bv_ref, sems):
+def state_kernel(parts, branch_ref, tk_hbm, tv_hbm, bk_hbm, bv_hbm, out_ref, tk_ref, tv_ref, bk_ref, bv_ref, sems):
     copies = [
         pltpu.make_async_copy(source, target, sems.at[i])
         for i, (source, target) in enumerate(
@@ -211,9 +211,12 @@
         middle = rest.astype(BF16)
         low = (rest - middle.astype(F32)).astype(BF16)
         keys, values = k_ref[...], v_ref[...]
-        kg_ref[...] = (dot(values, high, 1, 1) + (dot(values, middle, 1, 1) + dot(values, low, 1, 1))).astype(BF16)
+        twice = functools.partial(jnp.concatenate, axis=1)
+        most = dot(twice([values, values]), twice([high, middle]), 1, 1)
+        kg_ref[...] = (most + dot(values, low, 1, 1)).astype(BF16)
         copies[2 * i].start()
-        vg_ref[...] = (dot(keys, high) + (dot(keys, middle) + dot(keys, low))).astype(BF16)
+        most = dot(twice([keys, keys]), jnp.concatenate([high, middle], axis=0))
+        vg_ref[...] = (most + dot(keys, low)).astype(BF16)
         copies[2 * i + 1].start()
     for copy in copies:
         copy.wait()
@@ -227,10 +230,10 @@
     members = leaves // 2
     part = DH // members
     halves = [[h * members + i for i in range(members)] for h in range(2)]
-    near = 4
-    far = heads // near
-    near_groups = [[g * near + i for i in range(near)] for g in range(far)]
-    far_groups = [[i + near * g for g in range(far)] for i in range(near)]
+    wide_x, wide_y = 4, 8
+    plane = wide_x * wide_y
+    y_groups = [[z + y * wide_x + x for y in range(wide_y)] for z in range(0, heads, plane) for x in range(wide_x)]
+    xz_groups = [[z + y * wide_x + x for z in range(0, heads, plane) for x in range(wide_x)] for y in range(wide_y)]
     across = [(i, i ^ members) for i in range(leaves)]
     gain = norm_gain.reshape(1, DH)
 
@@ -243,9 +246,9 @@
         functools.partial(state_kernel, members),
         "state",
         [((members, 2 * part + 8, DH), F32)],
-        [SM] * 2 + [HB] * 4,
+        [SM] + [HB] * 4,
         scratch=[held] * 4 + [pltpu.SemaphoreType.DMA((4,))],
-    )(leaf_len, branch_id, *map(stay, (trunk_keys, trunk_values, branch_keys, branch_values)))
+    )(branch_id, *map(stay, (trunk_keys, trunk_values, branch_keys, branch_values)))
     got = exchange(sent, "leaf", halves)
     (half,) = call(functools.partial(half_sum_kernel, part), "half", [((2 * part, DH), F32)], [VM])(got)
     other = lax.ppermute(half, "leaf", across)
@@ -263,22 +266,22 @@
             ((blocks - 1, DH, DH), F32),
         ],
         [SM] + [VM] * 5 + [ANY],
-        flops=4 * rows * BLOCK * DH,
-        moved=6 * MIB,
+        flops=1000,
+        moved=1000,
     )(leaf_len, leaf_query, leaf_keys, leaf_values, out_grad, gain, half)
     (chunk,) = call(
         functools.partial(prefix_kernel, part, members), "prefix", [((members, part, DH), F32)], [VM] * 3 + [ANY]
     )(half, other, got, first)
     state = exchange(chunk, "leaf", halves)
     states, rawt, sums = call(
-        functools.partial(raw_kernel, near),
+        functools.partial(raw_kernel, wide_y),
         "raw",
-        [((blocks, DH, DH), BF16), ((DH, rows), F32), ((near, 2, rows), F32)],
+        [((blocks, DH, DH), BF16), ((DH, rows), F32), ((wide_y, 2, rows), F32)],
         [SM] + [VM] * 5,
     )(leaf_len, state, first, qt, lt, sgt)
-    sums = exchange(sums, "head", near_groups)
-    (sums,) = call(spread_kernel, "spread", [((far, 2, rows), F32)], [VM])(sums)
-    sums = exchange(sums, "head", far_groups)
+    sums = exchange(sums, "head", y_groups)
+    (sums,) = call(spread_kernel, "spread", [((len(xz_groups[0]), 2, rows), F32)], [VM])(sums)
+    sums = exchange(sums, "head", xz_groups)
     rgt, norm, later, sent = call(
         functools.partial(grad_kernel, heads * DH, members),
         "grad",

time: 116 us -> 115 us (level)
  waiting for transfers between devices: 5.65 us -> 3.56 us
    ppermute x1, waiting for transfers between devices: 4.8 us -> 3.56 us  [shards(): other = lax.ppermute(half, 'leaf', across)]
  transfers between devices with their start and end apart: 2 -> 2, of which waited for: 2 -> 1; matrix products, arithmetic and copies ran while one was open for 0% -> 0% of each run, Pallas kernels for 3% -> 3%
where the time goes in v3:
time: 115 us; the launch traced here: 114 us
  blocking collectives  92.2 us (80%)
  starting transfers between devices  8.64 us (8%)
  Pallas kernels  7.06 us (6%)
  waiting for transfers between devices  3.56 us (3%)
  between operations  2.1 us (2%)
    all_to_all x6, blocking collectives, exchange(): lax.all_to_all(value, axis, 0, 0, tiled=True, axis_index_groups=groups)  92.2 us
    ppermute x1, starting transfers between devices, shards(): other = lax.ppermute(own, 'leaf', across)  5.96 us
    ppermute x1, waiting for transfers between devices, shards(): other = lax.ppermute(half, 'leaf', across)  3.56 us
    ppermute x1, starting transfers between devices, shards(): other = lax.ppermute(half, 'leaf', across)  2.68 us
    pallas_call x1, Pallas kernels, shards(): call(leaf_kernel, 'leaf', [leaf] * 4 + [((8, DH), F32)], [VM] * 11 + [ANY...  2.65 us
  transfers between devices with their start and end apart: 2, of which 1 were waited for; matrix products, arithmetic and copies ran while one was open for 0% of the time, Pallas kernels for 3%

profile of v3, /device:TPU:1, one launch (start us, length us, event | category | flops | bytes accessed | tf_op | source)
XLA Modules:
  0.0 114.2 jit_solution(4753850683144756996)
XLA Ops:
  1.3 0.0 copy-start.5
  1.3 0.0 copy-start.6
  1.3 0.0 copy-start.7
  1.3 1.5 %state.1 = f32[8,40,128]{2,1,0:T(8,128)S(1)} custom-call(s32[1]{0:T(128)S(6)} %copy.20.branch_ref, bf16[512,128]{1,0:T(8,128)(2,1)} %tk_ref.1, bf16[512,128]{1,0:T(8,128)(2,1)} %tv_ref.1, bf16[512,128]{1,0:T(8,128)(2,1)} %bk_ref.1, bf16[512,128]{1,0:T(8,128)(2,1)} %bv_ref.1), custom_call_target="tpu_custom_call" | custom-call | flops 1000000 | bytes 1000000 | tf_op jit(solution)/shard_map/state/pallas_call | solution.py:245
  2.9 0.0 copy-start
  2.9 22.7 %all_to_all.30.in_ref.flags_ref = f32[8,40,128]{2,1,0:T(8,128)S(1)} all-to-all(f32[8,40,128]{2,1,0:T(8,128)S(1)} %state.1), channel_id=1, replica_groups={{0,64,128,192,256,320,384,448},{512,576,640,704,768,832,896,960},{1,65,..., dimensions={0} | all-to-all | bytes 327680 | tf_op jit(solution)/shard_map/all_to_all | solution.py:241
  25.6 2.7 %collective-permute-start = (f32[32,128]{1,0:T(8,128)S(1)}, f32[32,128]{1,0:T(8,128)S(1)}, u32[]{:S(2)}, u32[]{:S(2)}) collective-permute-start(f32[32,128]{1,0:T(8,128)S(1)} %half.1.after_ref.own_ref), channel_id=1, source_target_pairs={{0,512},{64,576},{128,640},{192,704},{256,768},{320,832},{384,896}... | collective-permute-start | bytes 49160 | tf_op jit(solution)/shard_map/ppermute | solution.py:254
  28.9 0.0 copy-start.8
  28.9 0.0 copy-done.5
  28.9 0.0 copy-done.6
  28.9 0.0 copy-done.7
  28.9 0.0 copy-done
  29.0 0.6 copy-done.8
  29.6 0.9 local.1
  30.5 3.6 %collective-permute-done.other_ref = f32[32,128]{1,0:T(8,128)S(1)} collective-permute-done((f32[32,128]{1,0:T(8,128)S(1)}, f32[32,128]{1,0:T(8,128)S(1)}, u32[]{:S(2)}, u32[]{:S(2)}) %collective-permute-start) | collective-permute-done | bytes 16416 | tf_op jit(solution)/shard_map/ppermute | solution.py:254
  34.0 10.0 %all_to_all.31.state_ref = f32[8,16,128]{2,1,0:T(8,128)S(1)} all-to-all(f32[8,16,128]{2,1,0:T(8,128)S(1)} %prefix.1), channel_id=1, replica_groups={{0,64,128,192,256,320,384,448},{512,576,640,704,768,832,896,960},{1,65,..., dimensions={0} | all-to-all | bytes 131072 | tf_op jit(solution)/shard_map/all_to_all | solution.py:241
  44.1 0.3 raw.1
  44.4 9.6 %all_to_all.32.in_ref = f32[8,2,1024]{2,1,0:T(2,128)S(1)} all-to-all(f32[8,2,1024]{2,1,0:T(2,128)S(1)} %get-tuple-element.40), channel_id=1, replica_groups={{0,4,8,12,16,20,24,28},{1,5,9,13,17,21,25,29},{2,6,10,14,18,22,26,30},{..., dimensions={0} | all-to-all | bytes 131072 | tf_op jit(solution)/shard_map/all_to_all | solution.py:241
  54.0 28.2 %all_to_all.33.sums_ref = f32[8,2,1024]{2,1,0:T(2,128)S(1)} all-to-all(f32[8,2,1024]{2,1,0:T(2,128)S(1)} %spread.1), channel_id=1, replica_groups={{0,1,2,3,32,33,34,35},{4,5,6,7,36,37,38,39},{8,9,10,11,40,41,42,43},{12..., dimensions={0} | all-to-all | bytes 131072 | tf_op jit(solution)/shard_map/all_to_all | solution.py:241
  82.3 0.3 grad.1
  82.5 11.2 %all_to_all.34.in_ref = f32[8,16,128]{2,1,0:T(8,128)S(1)} all-to-all(f32[8,16,128]{2,1,0:T(8,128)S(1)} %get-tuple-element.46), channel_id=1, replica_groups={{0,64,128,192,256,320,384,448},{512,576,640,704,768,832,896,960},{1,65,..., dimensions={0} | all-to-all | bytes 131072 | tf_op jit(solution)/shard_map/all_to_all | solution.py:241
  93.7 6.0 %collective-permute-start.1 = (f32[32,128]{1,0:T(8,128)S(1)}, f32[32,128]{1,0:T(8,128)S(1)}, u32[]{:S(2)}, u32[]{:S(2)}) collective-permute-start(f32[32,128]{1,0:T(8,128)S(1)} %by_branch.1.after_ref.own_ref), channel_id=1, source_target_pairs={{0,512},{64,576},{128,640},{192,704},{256,768},{320,832},{384,896}... | collective-permute-start | bytes 49160 | tf_op jit(solution)/shard_map/ppermute | solution.py:294
  99.7 0.0 copy-start.4
  99.7 2.7 %leaf.1 = (bf16[1024,128]{1,0:T(8,128)(2,1)}, bf16[1024,128]{1,0:T(8,128)(2,1)}, bf16[1024,128]{1,0:T(8,128)(2,1)}, bf16[1024,128]{1,0:T(8,128)(2,1)}, f32[8,128]{1,0:T(8,128)S(1)}) custom-call(bf16[1024,128]{1,0:T(8,128)(2,1)S(1)} %copy-done, bf16[1024,128]{1,0:T(8,128)(2,1)S(1)} %get-tuple-element.32.km_ref, ...), custom_call_target="tpu_custom_call" | custom-call | flops 536870912 | bytes 6291456 | tf_op jit(solution)/shard_map/leaf/pallas_call | solution.py:295
  102.4 0.0 collective-permute-done.1.other_ref
  102.4 0.0 copy-start.3
  102.4 0.0 copy-start.1
  102.4 0.0 copy-start.2
  102.4 10.5 %all_to_all.35.in_ref = f32[8,32,128]{2,1,0:T(8,128)S(1)} all-to-all(f32[8,32,128]{2,1,0:T(8,128)S(1)} %total.1), channel_id=1, replica_groups={{0,64,128,192,256,320,384,448},{512,576,640,704,768,832,896,960},{1,65,..., dimensions={0} | all-to-all | bytes 262144 | tf_op jit(solution)/shard_map/all_to_all | solution.py:241
  112.9 0.0 copy-done.4
  112.9 0.0 copy-done.3
  112.9 0.0 copy-done.1
  112.9 0.0 copy-done.2
  112.9 1.3 %tree.1 = (bf16[512,128]{1,0:T(8,128)(2,1)}, bf16[512,128]{1,0:T(8,128)(2,1)}, bf16[512,128]{1,0:T(8,128)(2,1)}, bf16[512,128]{1,0:T(8,128)(2,1)}) custom-call(f32[8,32,128]{2,1,0:T(8,128)S(1)} %all_to_all.35.in_ref, bf16[512,128]{1,0:T(8,128)(2,1)S(1)} %copy-done.1, bf16[512,128]{1,0:T(8,128)(2,1)S(1)} %copy-done.2, bf16[512,128]{1,0:T(8,128)(2,1)S(1)} %copy-done.3, ...), custom_call_target="tpu_custom_call" | custom-call | flops 1000000 | bytes 1000000 | tf_op jit(solution)/shard_map/tree/pallas_call | solution.py:303
  (5 shorter events, 0.1 us)
Async XLA Ops:
  1.3 27.6 %copy-start.5 = (bf16[1024,128]{1,0:T(8,128)(2,1)S(1)}, bf16[1024,128]{1,0:T(8,128)(2,1)}, u32[]{:S(2)}) copy-start(bf16[1024,128]{1,0:T(8,128)(2,1)} %k_ref.1) | copy-start | bytes 786436
  1.3 27.6 %copy-start.6 = (bf16[1024,128]{1,0:T(8,128)(2,1)S(1)}, bf16[1024,128]{1,0:T(8,128)(2,1)}, u32[]{:S(2)}) copy-start(bf16[1024,128]{1,0:T(8,128)(2,1)} %v_ref.1) | copy-start | bytes 786436
  1.3 27.6 %copy-start.7 = (bf16[1024,128]{1,0:T(8,128)(2,1)S(1)}, bf16[1024,128]{1,0:T(8,128)(2,1)}, u32[]{:S(2)}) copy-start(bf16[1024,128]{1,0:T(8,128)(2,1)} %g_ref.1) | copy-start | bytes 786436
  2.9 26.1 %copy-start = (bf16[1024,128]{1,0:T(8,128)(2,1)S(1)}, bf16[1024,128]{1,0:T(8,128)(2,1)}, u32[]{:S(2)}) copy-start(bf16[1024,128]{1,0:T(8,128)(2,1)} %q_ref.3) | copy-start | bytes 786436
  25.6 8.5 %collective-permute-start = (f32[32,128]{1,0:T(8,128)S(1)}, f32[32,128]{1,0:T(8,128)S(1)}, u32[]{:S(2)}, u32[]{:S(2)}) collective-permute-start(f32[32,128]{1,0:T(8,128)S(1)} %half.1.after_ref.own_ref), channel_id=1, source_target_pairs={{0,512},{64,576},{128,640},{192,704},{256,768},{320,832},{384,896}... | collective-permute-start | bytes 49160 | tf_op jit(solution)/shard_map/ppermute | solution.py:254
  28.9 0.7 copy-start.8
  93.7 8.6 %collective-permute-start.1 = (f32[32,128]{1,0:T(8,128)S(1)}, f32[32,128]{1,0:T(8,128)S(1)}, u32[]{:S(2)}, u32[]{:S(2)}) collective-permute-start(f32[32,128]{1,0:T(8,128)S(1)} %by_branch.1.after_ref.own_ref), channel_id=1, source_target_pairs={{0,512},{64,576},{128,640},{192,704},{256,768},{320,832},{384,896}... | collective-permute-start | bytes 49160 | tf_op jit(solution)/shard_map/ppermute | solution.py:294
  99.7 13.2 %copy-start.4 = (bf16[512,128]{1,0:T(8,128)(2,1)S(1)}, bf16[512,128]{1,0:T(8,128)(2,1)}, u32[]{:S(2)}) copy-start(bf16[512,128]{1,0:T(8,128)(2,1)} %bv_ref.1) | copy-start | bytes 393220
  102.4 10.6 %copy-start.3 = (bf16[512,128]{1,0:T(8,128)(2,1)S(1)}, bf16[512,128]{1,0:T(8,128)(2,1)}, u32[]{:S(2)}) copy-start(bf16[512,128]{1,0:T(8,128)(2,1)} %bk_ref.1) | copy-start | bytes 393220
  102.4 10.5 %copy-start.1 = (bf16[512,128]{1,0:T(8,128)(2,1)S(1)}, bf16[512,128]{1,0:T(8,128)(2,1)}, u32[]{:S(2)}) copy-start(bf16[512,128]{1,0:T(8,128)(2,1)} %tk_ref.1) | copy-start | bytes 393220
  102.4 10.5 %copy-start.2 = (bf16[512,128]{1,0:T(8,128)(2,1)S(1)}, bf16[512,128]{1,0:T(8,128)(2,1)}, u32[]{:S(2)}) copy-start(bf16[512,128]{1,0:T(8,128)(2,1)} %tv_ref.1) | copy-start | bytes 393220

commit v4 on v3

--- a/solution.py
+++ b/solution.py
@@ -13,6 +13,7 @@
 F32 = jnp.float32
 BF16 = jnp.bfloat16
 MIB = 1 << 20
+LEAD = 5
 
 VM = pl.BlockSpec(memory_space=pltpu.VMEM)
 SM = pl.BlockSpec(memory_space=pltpu.SMEM)
@@ -222,6 +223,10 @@
         copy.wait()
 
 
+def led_by(members, lead):
+    return [lead] + [i for i in members if i != lead]
+
+
 def shards(mesh_shape, leaf_query, leaf_keys, leaf_values, out_grad, leaf_len, branch_id, trunk_keys, trunk_values, branch_keys, branch_values, norm_gain):
     leaves, heads = mesh_shape
     rows = leaf_query.shape[0]
@@ -229,11 +234,14 @@
     blocks = rows // BLOCK
     members = leaves // 2
     part = DH // members
-    halves = [[h * members + i for i in range(members)] for h in range(2)]
+    order = led_by(range(members), LEAD)
+    halves = [[h * members + i for i in order] for h in range(2)]
     wide_x, wide_y = 4, 8
     plane = wide_x * wide_y
-    y_groups = [[z + y * wide_x + x for y in range(wide_y)] for z in range(0, heads, plane) for x in range(wide_x)]
-    xz_groups = [[z + y * wide_x + x for z in range(0, heads, plane) for x in range(wide_x)] for y in range(wide_y)]
+    y_order = led_by(range(wide_y), wide_y // 2)
+    xz_order = led_by([z + x for z in range(0, heads, plane) for x in range(wide_x)], heads - plane + wide_x // 2)
+    y_groups = [[z + y * wide_x + x for y in y_order] for z in range(0, heads, plane) for x in range(wide_x)]
+    xz_groups = [[i + y * wide_x for i in xz_order] for y in range(wide_y)]
     across = [(i, i ^ members) for i in range(leaves)]
     gain = norm_gain.reshape(1, DH)
 

time: 115 us -> 97.2 us (0.85)
  blocking collectives: 92.2 us -> 74.4 us
  waiting for transfers between devices: 3.56 us -> 6.88 us
  starting transfers between devices: 8.64 us -> 5.63 us
    all_to_all x6, blocking collectives: 92.2 us -> 74.4 us  [exchange(): lax.all_to_all(value, axis, 0, 0, tiled=True, axis_index_groups=groups)]
    ppermute x1, starting transfers between devices: 5.96 us -> 3.71 us  [shards(): other = lax.ppermute(own, 'leaf', across)]
    ppermute x1, waiting for transfers between devices: 0.01 us -> 2.13 us  [shards(): other = lax.ppermute(own, 'leaf', across)]
    ppermute x1, waiting for transfers between devices: 3.56 us -> 4.75 us  [shards(): other = lax.ppermute(half, 'leaf', across)]
  transfers between devices with their start and end apart: 2 -> 2, of which waited for: 1 -> 2; matrix products, arithmetic and copies ran while one was open for 0% -> 0% of each run, Pallas kernels for 3% -> 4%
where the time goes in v4:
time: 97.2 us; the launch traced here: 96.7 us
  blocking collectives  74.4 us (77%)
  Pallas kernels  7.07 us (7%)
  waiting for transfers between devices  6.88 us (7%)
  starting transfers between devices  5.63 us (6%)
  between operations  2.1 us (2%)
    all_to_all x6, blocking collectives, exchange(): lax.all_to_all(value, axis, 0, 0, tiled=True, axis_index_groups=groups)  74.4 us
    ppermute x1, waiting for transfers between devices, shards(): other = lax.ppermute(half, 'leaf', across)  4.75 us
    ppermute x1, starting transfers between devices, shards(): other = lax.ppermute(own, 'leaf', across)  3.71 us
    pallas_call x1, Pallas kernels, shards(): call(leaf_kernel, 'leaf', [leaf] * 4 + [((8, DH), F32)], [VM] * 11 + [ANY...  2.65 us
    ppermute x1, waiting for transfers between devices, shards(): other = lax.ppermute(own, 'leaf', across)  2.13 us
  transfers between devices with their start and end apart: 2, of which 2 were waited for; matrix products, arithmetic and copies ran while one was open for 0% of the time, Pallas kernels for 4%

profile of v4, /device:TPU:1, one launch (start us, length us, event | category | flops | bytes accessed | tf_op | source)
XLA Modules:
  0.0 96.7 jit_solution(15004584945227932604)
XLA Ops:
  1.3 0.0 copy-start.5
  1.3 0.0 copy-start.6
  1.3 0.0 copy-start.7
  1.3 1.5 %state.1 = f32[8,40,128]{2,1,0:T(8,128)S(1)} custom-call(s32[1]{0:T(128)S(6)} %copy.20.branch_ref, bf16[512,128]{1,0:T(8,128)(2,1)} %tk_ref.1, bf16[512,128]{1,0:T(8,128)(2,1)} %tv_ref.1, bf16[512,128]{1,0:T(8,128)(2,1)} %bk_ref.1, bf16[512,128]{1,0:T(8,128)(2,1)} %bv_ref.1), custom_call_target="tpu_custom_call" | custom-call | flops 1000000 | bytes 1000000 | tf_op jit(solution)/shard_map/state/pallas_call | solution.py:253
  2.9 0.0 copy-start
  2.9 22.5 %all_to_all.30.in_ref.flags_ref = f32[8,40,128]{2,1,0:T(8,128)S(1)} all-to-all(f32[8,40,128]{2,1,0:T(8,128)S(1)} %state.1), channel_id=1, replica_groups={{320,0,64,128,192,256,384,448},{832,512,576,640,704,768,896,960},{321,1..., dimensions={0} | all-to-all | bytes 327680 | tf_op jit(solution)/shard_map/all_to_all | solution.py:249
  25.4 1.9 %collective-permute-start = (f32[32,128]{1,0:T(8,128)S(1)}, f32[32,128]{1,0:T(8,128)S(1)}, u32[]{:S(2)}, u32[]{:S(2)}) collective-permute-start(f32[32,128]{1,0:T(8,128)S(1)} %half.1.after_ref.own_ref), channel_id=1, source_target_pairs={{0,512},{64,576},{128,640},{192,704},{256,768},{320,832},{384,896}... | collective-permute-start | bytes 49160 | tf_op jit(solution)/shard_map/ppermute | solution.py:262
  28.0 0.0 copy-start.8
  28.0 0.0 copy-done.5
  28.0 0.0 copy-done.6
  28.0 0.0 copy-done.7
  28.0 0.0 copy-done
  28.0 0.6 copy-done.8
  28.7 0.9 local.1
  29.6 4.8 %collective-permute-done.other_ref = f32[32,128]{1,0:T(8,128)S(1)} collective-permute-done((f32[32,128]{1,0:T(8,128)S(1)}, f32[32,128]{1,0:T(8,128)S(1)}, u32[]{:S(2)}, u32[]{:S(2)}) %collective-permute-start) | collective-permute-done | bytes 16416 | tf_op jit(solution)/shard_map/ppermute | solution.py:262
  34.3 7.9 %all_to_all.31.state_ref = f32[8,16,128]{2,1,0:T(8,128)S(1)} all-to-all(f32[8,16,128]{2,1,0:T(8,128)S(1)} %prefix.1), channel_id=1, replica_groups={{320,0,64,128,192,256,384,448},{832,512,576,640,704,768,896,960},{321,1..., dimensions={0} | all-to-all | bytes 131072 | tf_op jit(solution)/shard_map/all_to_all | solution.py:249
  42.2 0.3 raw.1
  42.5 8.7 %all_to_all.32.in_ref = f32[8,2,1024]{2,1,0:T(2,128)S(1)} all-to-all(f32[8,2,1024]{2,1,0:T(2,128)S(1)} %get-tuple-element.40), channel_id=1, replica_groups={{16,0,4,8,12,20,24,28},{17,1,5,9,13,21,25,29},{18,2,6,10,14,22,26,30},{..., dimensions={0} | all-to-all | bytes 131072 | tf_op jit(solution)/shard_map/all_to_all | solution.py:249
  51.2 15.5 %all_to_all.33.sums_ref = f32[8,2,1024]{2,1,0:T(2,128)S(1)} all-to-all(f32[8,2,1024]{2,1,0:T(2,128)S(1)} %spread.1), channel_id=1, replica_groups={{34,0,1,2,3,32,33,35},{38,4,5,6,7,36,37,39},{42,8,9,10,11,40,41,43},{46..., dimensions={0} | all-to-all | bytes 131072 | tf_op jit(solution)/shard_map/all_to_all | solution.py:249
  66.8 0.3 grad.1
  67.1 10.2 %all_to_all.34.in_ref = f32[8,16,128]{2,1,0:T(8,128)S(1)} all-to-all(f32[8,16,128]{2,1,0:T(8,128)S(1)} %get-tuple-element.46), channel_id=1, replica_groups={{320,0,64,128,192,256,384,448},{832,512,576,640,704,768,896,960},{321,1..., dimensions={0} | all-to-all | bytes 131072 | tf_op jit(solution)/shard_map/all_to_all | solution.py:249
  77.3 3.7 %collective-permute-start.1 = (f32[32,128]{1,0:T(8,128)S(1)}, f32[32,128]{1,0:T(8,128)S(1)}, u32[]{:S(2)}, u32[]{:S(2)}) collective-permute-start(f32[32,128]{1,0:T(8,128)S(1)} %by_branch.1.after_ref.own_ref), channel_id=1, source_target_pairs={{0,512},{64,576},{128,640},{192,704},{256,768},{320,832},{384,896}... | collective-permute-start | bytes 49160 | tf_op jit(solution)/shard_map/ppermute | solution.py:302
  81.0 0.0 copy-start.4
  81.0 2.7 %leaf.1 = (bf16[1024,128]{1,0:T(8,128)(2,1)}, bf16[1024,128]{1,0:T(8,128)(2,1)}, bf16[1024,128]{1,0:T(8,128)(2,1)}, bf16[1024,128]{1,0:T(8,128)(2,1)}, f32[8,128]{1,0:T(8,128)S(1)}) custom-call(bf16[1024,128]{1,0:T(8,128)(2,1)S(1)} %copy-done, bf16[1024,128]{1,0:T(8,128)(2,1)S(1)} %get-tuple-element.32.km_ref, ...), custom_call_target="tpu_custom_call" | custom-call | flops 536870912 | bytes 6291456 | tf_op jit(solution)/shard_map/leaf/pallas_call | solution.py:303
  83.7 2.1 %collective-permute-done.1.other_ref = f32[32,128]{1,0:T(8,128)S(1)} collective-permute-done((f32[32,128]{1,0:T(8,128)S(1)}, f32[32,128]{1,0:T(8,128)S(1)}, u32[]{:S(2)}, u32[]{:S(2)}) %collective-permute-start.1) | collective-permute-done | bytes 16416 | tf_op jit(solution)/shard_map/ppermute | solution.py:302
  85.8 0.0 copy-start.3
  85.8 0.0 copy-start.1
  85.9 0.0 copy-start.2
  85.9 9.5 %all_to_all.35.in_ref = f32[8,32,128]{2,1,0:T(8,128)S(1)} all-to-all(f32[8,32,128]{2,1,0:T(8,128)S(1)} %total.1), channel_id=1, replica_groups={{320,0,64,128,192,256,384,448},{832,512,576,640,704,768,896,960},{321,1..., dimensions={0} | all-to-all | bytes 262144 | tf_op jit(solution)/shard_map/all_to_all | solution.py:249
  95.4 0.0 copy-done.4
  95.4 0.0 copy-done.3
  95.4 0.0 copy-done.1
  95.4 0.0 copy-done.2
  95.4 1.3 %tree.1 = (bf16[512,128]{1,0:T(8,128)(2,1)}, bf16[512,128]{1,0:T(8,128)(2,1)}, bf16[512,128]{1,0:T(8,128)(2,1)}, bf16[512,128]{1,0:T(8,128)(2,1)}) custom-call(f32[8,32,128]{2,1,0:T(8,128)S(1)} %all_to_all.35.in_ref, bf16[512,128]{1,0:T(8,128)(2,1)S(1)} %copy-done.1, bf16[512,128]{1,0:T(8,128)(2,1)S(1)} %copy-done.2, bf16[512,128]{1,0:T(8,128)(2,1)S(1)} %copy-done.3, ...), custom_call_target="tpu_custom_call" | custom-call | flops 1000000 | bytes 1000000 | tf_op jit(solution)/shard_map/tree/pallas_call | solution.py:311
  (5 shorter events, 0.1 us)
Async XLA Ops:
  1.3 26.7 %copy-start.5 = (bf16[1024,128]{1,0:T(8,128)(2,1)S(1)}, bf16[1024,128]{1,0:T(8,128)(2,1)}, u32[]{:S(2)}) copy-start(bf16[1024,128]{1,0:T(8,128)(2,1)} %k_ref.1) | copy-start | bytes 786436
  1.3 26.7 %copy-start.6 = (bf16[1024,128]{1,0:T(8,128)(2,1)S(1)}, bf16[1024,128]{1,0:T(8,128)(2,1)}, u32[]{:S(2)}) copy-start(bf16[1024,128]{1,0:T(8,128)(2,1)} %v_ref.1) | copy-start | bytes 786436
  1.3 26.7 %copy-start.7 = (bf16[1024,128]{1,0:T(8,128)(2,1)S(1)}, bf16[1024,128]{1,0:T(8,128)(2,1)}, u32[]{:S(2)}) copy-start(bf16[1024,128]{1,0:T(8,128)(2,1)} %g_ref.1) | copy-start | bytes 786436
  2.9 25.2 %copy-start = (bf16[1024,128]{1,0:T(8,128)(2,1)S(1)}, bf16[1024,128]{1,0:T(8,128)(2,1)}, u32[]{:S(2)}) copy-start(bf16[1024,128]{1,0:T(8,128)(2,1)} %q_ref.3) | copy-start | bytes 786436
  25.4 8.9 %collective-permute-start = (f32[32,128]{1,0:T(8,128)S(1)}, f32[32,128]{1,0:T(8,128)S(1)}, u32[]{:S(2)}, u32[]{:S(2)}) collective-permute-start(f32[32,128]{1,0:T(8,128)S(1)} %half.1.after_ref.own_ref), channel_id=1, source_target_pairs={{0,512},{64,576},{128,640},{192,704},{256,768},{320,832},{384,896}... | collective-permute-start | bytes 49160 | tf_op jit(solution)/shard_map/ppermute | solution.py:262
  28.0 0.7 copy-start.8
  77.3 8.5 %collective-permute-start.1 = (f32[32,128]{1,0:T(8,128)S(1)}, f32[32,128]{1,0:T(8,128)S(1)}, u32[]{:S(2)}, u32[]{:S(2)}) collective-permute-start(f32[32,128]{1,0:T(8,128)S(1)} %by_branch.1.after_ref.own_ref), channel_id=1, source_target_pairs={{0,512},{64,576},{128,640},{192,704},{256,768},{320,832},{384,896}... | collective-permute-start | bytes 49160 | tf_op jit(solution)/shard_map/ppermute | solution.py:302
  81.0 14.4 %copy-start.4 = (bf16[512,128]{1,0:T(8,128)(2,1)S(1)}, bf16[512,128]{1,0:T(8,128)(2,1)}, u32[]{:S(2)}) copy-start(bf16[512,128]{1,0:T(8,128)(2,1)} %bv_ref.1) | copy-start | bytes 393220
  85.8 9.6 %copy-start.3 = (bf16[512,128]{1,0:T(8,128)(2,1)S(1)}, bf16[512,128]{1,0:T(8,128)(2,1)}, u32[]{:S(2)}) copy-start(bf16[512,128]{1,0:T(8,128)(2,1)} %bk_ref.1) | copy-start | bytes 393220
  85.8 9.6 %copy-start.1 = (bf16[512,128]{1,0:T(8,128)(2,1)S(1)}, bf16[512,128]{1,0:T(8,128)(2,1)}, u32[]{:S(2)}) copy-start(bf16[512,128]{1,0:T(8,128)(2,1)} %tk_ref.1) | copy-start | bytes 393220
  85.9 9.6 %copy-start.2 = (bf16[512,128]{1,0:T(8,128)(2,1)S(1)}, bf16[512,128]{1,0:T(8,128)(2,1)}, u32[]{:S(2)}) copy-start(bf16[512,128]{1,0:T(8,128)(2,1)} %tv_ref.1) | copy-start | bytes 393220

commit v5 on v4

--- a/solution.py
+++ b/solution.py
@@ -13,7 +13,7 @@
 F32 = jnp.float32
 BF16 = jnp.bfloat16
 MIB = 1 << 20
-LEAD = 5
+LEAD = 3
 
 VM = pl.BlockSpec(memory_space=pltpu.VMEM)
 SM = pl.BlockSpec(memory_space=pltpu.SMEM)
@@ -238,8 +238,8 @@
     halves = [[h * members + i for i in order] for h in range(2)]
     wide_x, wide_y = 4, 8
     plane = wide_x * wide_y
-    y_order = led_by(range(wide_y), wide_y // 2)
-    xz_order = led_by([z + x for z in range(0, heads, plane) for x in range(wide_x)], heads - plane + wide_x // 2)
+    y_order = led_by(range(wide_y), 0)
+    xz_order = led_by([z + x for z in range(0, heads, plane) for x in range(wide_x)], heads - plane)
     y_groups = [[z + y * wide_x + x for y in y_order] for z in range(0, heads, plane) for x in range(wide_x)]
     xz_groups = [[i + y * wide_x for i in xz_order] for y in range(wide_y)]
     across = [(i, i ^ members) for i in range(leaves)]

time: 97.2 us -> 101 us (1.039)
  blocking collectives: 74.4 us -> 77.8 us
  starting transfers between devices: 5.63 us -> 8.54 us
  waiting for transfers between devices: 6.88 us -> 4.57 us
    all_to_all x6, blocking collectives: 74.4 us -> 77.8 us  [exchange(): lax.all_to_all(value, axis, 0, 0, tiled=True, axis_index_groups=groups)]
    ppermute x1, starting transfers between devices: 3.71 us -> 6 us  [shards(): other = lax.ppermute(own, 'leaf', across)]
    ppermute x1, waiting for transfers between devices: 2.13 us -> 0.01 us  [shards(): other = lax.ppermute(own, 'leaf', across)]
  transfers between devices with their start and end apart: 2 -> 2, of which waited for: 2 -> 1; matrix products, arithmetic and copies ran while one was open for 0% -> 0% of each run, Pallas kernels for 4% -> 4%
where the time goes in v5:
time: 101 us
  blocking collectives  77.8 us (77%)
  starting transfers between devices  8.54 us (8%)
  Pallas kernels  7.06 us (7%)
  waiting for transfers between devices  4.57 us (5%)
  between operations  2.1 us (2%)
    all_to_all x6, blocking collectives, exchange(): lax.all_to_all(value, axis, 0, 0, tiled=True, axis_index_groups=groups)  77.8 us
    ppermute x1, starting transfers between devices, shards(): other = lax.ppermute(own, 'leaf', across)  6 us
    ppermute x1, waiting for transfers between devices, shards(): other = lax.ppermute(half, 'leaf', across)  4.57 us
    pallas_call x1, Pallas kernels, shards(): call(leaf_kernel, 'leaf', [leaf] * 4 + [((8, DH), F32)], [VM] * 11 + [ANY...  2.65 us
    ppermute x1, starting transfers between devices, shards(): other = lax.ppermute(half, 'leaf', across)  2.54 us
  transfers between devices with their start and end apart: 2, of which 1 were waited for; matrix products, arithmetic and copies ran while one was open for 0% of the time, Pallas kernels for 4%

profile of v5, /device:TPU:1, one launch (start us, length us, event | category | flops | bytes accessed | tf_op | source)
XLA Modules:
  0.0 100.7 jit_solution(3575019901172074765)
XLA Ops:
  1.3 0.0 copy-start.5
  1.3 0.0 copy-start.6
  1.3 0.0 copy-start.7
  1.3 1.5 %state.1 = f32[8,40,128]{2,1,0:T(8,128)S(1)} custom-call(s32[1]{0:T(128)S(6)} %copy.20.branch_ref, bf16[512,128]{1,0:T(8,128)(2,1)} %tk_ref.1, bf16[512,128]{1,0:T(8,128)(2,1)} %tv_ref.1, bf16[512,128]{1,0:T(8,128)(2,1)} %bk_ref.1, bf16[512,128]{1,0:T(8,128)(2,1)} %bv_ref.1), custom_call_target="tpu_custom_call" | custom-call | flops 1000000 | bytes 1000000 | tf_op jit(solution)/shard_map/state/pallas_call | solution.py:253
  2.9 0.0 copy-start
  2.9 22.5 %all_to_all.30.in_ref.flags_ref = f32[8,40,128]{2,1,0:T(8,128)S(1)} all-to-all(f32[8,40,128]{2,1,0:T(8,128)S(1)} %state.1), channel_id=1, replica_groups={{192,0,64,128,256,320,384,448},{704,512,576,640,768,832,896,960},{193,1..., dimensions={0} | all-to-all | bytes 327680 | tf_op jit(solution)/shard_map/all_to_all | solution.py:249
  25.4 2.5 %collective-permute-start = (f32[32,128]{1,0:T(8,128)S(1)}, f32[32,128]{1,0:T(8,128)S(1)}, u32[]{:S(2)}, u32[]{:S(2)}) collective-permute-start(f32[32,128]{1,0:T(8,128)S(1)} %half.1.after_ref.own_ref), channel_id=1, source_target_pairs={{0,512},{64,576},{128,640},{192,704},{256,768},{320,832},{384,896}... | collective-permute-start | bytes 49160 | tf_op jit(solution)/shard_map/ppermute | solution.py:262
  28.6 0.0 copy-start.8
  28.6 0.0 copy-done.5
  28.6 0.0 copy-done.6
  28.6 0.0 copy-done.7
  28.7 0.0 copy-done
  28.7 0.6 copy-done.8
  29.3 0.9 local.1
  30.2 4.6 %collective-permute-done.other_ref = f32[32,128]{1,0:T(8,128)S(1)} collective-permute-done((f32[32,128]{1,0:T(8,128)S(1)}, f32[32,128]{1,0:T(8,128)S(1)}, u32[]{:S(2)}, u32[]{:S(2)}) %collective-permute-start) | collective-permute-done | bytes 16416 | tf_op jit(solution)/shard_map/ppermute | solution.py:262
  34.8 7.4 %all_to_all.31.state_ref = f32[8,16,128]{2,1,0:T(8,128)S(1)} all-to-all(f32[8,16,128]{2,1,0:T(8,128)S(1)} %prefix.1), channel_id=1, replica_groups={{192,0,64,128,256,320,384,448},{704,512,576,640,768,832,896,960},{193,1..., dimensions={0} | all-to-all | bytes 131072 | tf_op jit(solution)/shard_map/all_to_all | solution.py:249
  42.2 0.3 raw.1
  42.5 9.5 %all_to_all.32.in_ref = f32[8,2,1024]{2,1,0:T(2,128)S(1)} all-to-all(f32[8,2,1024]{2,1,0:T(2,128)S(1)} %get-tuple-element.40), channel_id=1, replica_groups={{0,4,8,12,16,20,24,28},{1,5,9,13,17,21,25,29},{2,6,10,14,18,22,26,30},{..., dimensions={0} | all-to-all | bytes 131072 | tf_op jit(solution)/shard_map/all_to_all | solution.py:249
  52.1 18.8 %all_to_all.33.sums_ref = f32[8,2,1024]{2,1,0:T(2,128)S(1)} all-to-all(f32[8,2,1024]{2,1,0:T(2,128)S(1)} %spread.1), channel_id=1, replica_groups={{32,0,1,2,3,33,34,35},{36,4,5,6,7,37,38,39},{40,8,9,10,11,41,42,43},{44..., dimensions={0} | all-to-all | bytes 131072 | tf_op jit(solution)/shard_map/all_to_all | solution.py:249
  70.8 0.3 grad.1
  71.1 10.1 %all_to_all.34.in_ref = f32[8,16,128]{2,1,0:T(8,128)S(1)} all-to-all(f32[8,16,128]{2,1,0:T(8,128)S(1)} %get-tuple-element.46), channel_id=1, replica_groups={{192,0,64,128,256,320,384,448},{704,512,576,640,768,832,896,960},{193,1..., dimensions={0} | all-to-all | bytes 131072 | tf_op jit(solution)/shard_map/all_to_all | solution.py:249
  81.2 6.0 %collective-permute-start.1 = (f32[32,128]{1,0:T(8,128)S(1)}, f32[32,128]{1,0:T(8,128)S(1)}, u32[]{:S(2)}, u32[]{:S(2)}) collective-permute-start(f32[32,128]{1,0:T(8,128)S(1)} %by_branch.1.after_ref.own_ref), channel_id=1, source_target_pairs={{0,512},{64,576},{128,640},{192,704},{256,768},{320,832},{384,896}... | collective-permute-start | bytes 49160 | tf_op jit(solution)/shard_map/ppermute | solution.py:302
  87.2 0.0 copy-start.4
  87.2 2.7 %leaf.1 = (bf16[1024,128]{1,0:T(8,128)(2,1)}, bf16[1024,128]{1,0:T(8,128)(2,1)}, bf16[1024,128]{1,0:T(8,128)(2,1)}, bf16[1024,128]{1,0:T(8,128)(2,1)}, f32[8,128]{1,0:T(8,128)S(1)}) custom-call(bf16[1024,128]{1,0:T(8,128)(2,1)S(1)} %copy-done, bf16[1024,128]{1,0:T(8,128)(2,1)S(1)} %get-tuple-element.32.km_ref, ...), custom_call_target="tpu_custom_call" | custom-call | flops 536870912 | bytes 6291456 | tf_op jit(solution)/shard_map/leaf/pallas_call | solution.py:303
  89.9 0.0 collective-permute-done.1.other_ref
  89.9 0.0 copy-start.3
  89.9 0.0 copy-start.1
  89.9 0.0 copy-start.2
  89.9 9.5 %all_to_all.35.in_ref = f32[8,32,128]{2,1,0:T(8,128)S(1)} all-to-all(f32[8,32,128]{2,1,0:T(8,128)S(1)} %total.1), channel_id=1, replica_groups={{192,0,64,128,256,320,384,448},{704,512,576,640,768,832,896,960},{193,1..., dimensions={0} | all-to-all | bytes 262144 | tf_op jit(solution)/shard_map/all_to_all | solution.py:249
  99.4 0.0 copy-done.4
  99.4 0.0 copy-done.3
  99.4 0.0 copy-done.1
  99.4 0.0 copy-done.2
  99.4 1.3 %tree.1 = (bf16[512,128]{1,0:T(8,128)(2,1)}, bf16[512,128]{1,0:T(8,128)(2,1)}, bf16[512,128]{1,0:T(8,128)(2,1)}, bf16[512,128]{1,0:T(8,128)(2,1)}) custom-call(f32[8,32,128]{2,1,0:T(8,128)S(1)} %all_to_all.35.in_ref, bf16[512,128]{1,0:T(8,128)(2,1)S(1)} %copy-done.1, bf16[512,128]{1,0:T(8,128)(2,1)S(1)} %copy-done.2, bf16[512,128]{1,0:T(8,128)(2,1)S(1)} %copy-done.3, ...), custom_call_target="tpu_custom_call" | custom-call | flops 1000000 | bytes 1000000 | tf_op jit(solution)/shard_map/tree/pallas_call | solution.py:311
  (5 shorter events, 0.1 us)
Async XLA Ops:
  1.3 27.4 %copy-start.5 = (bf16[1024,128]{1,0:T(8,128)(2,1)S(1)}, bf16[1024,128]{1,0:T(8,128)(2,1)}, u32[]{:S(2)}) copy-start(bf16[1024,128]{1,0:T(8,128)(2,1)} %k_ref.1) | copy-start | bytes 786436
  1.3 27.4 %copy-start.6 = (bf16[1024,128]{1,0:T(8,128)(2,1)S(1)}, bf16[1024,128]{1,0:T(8,128)(2,1)}, u32[]{:S(2)}) copy-start(bf16[1024,128]{1,0:T(8,128)(2,1)} %v_ref.1) | copy-start | bytes 786436
  1.3 27.4 %copy-start.7 = (bf16[1024,128]{1,0:T(8,128)(2,1)S(1)}, bf16[1024,128]{1,0:T(8,128)(2,1)}, u32[]{:S(2)}) copy-start(bf16[1024,128]{1,0:T(8,128)(2,1)} %g_ref.1) | copy-start | bytes 786436
  2.9 25.8 %copy-start = (bf16[1024,128]{1,0:T(8,128)(2,1)S(1)}, bf16[1024,128]{1,0:T(8,128)(2,1)}, u32[]{:S(2)}) copy-start(bf16[1024,128]{1,0:T(8,128)(2,1)} %q_ref.3) | copy-start | bytes 786436
  25.4 9.3 %collective-permute-start = (f32[32,128]{1,0:T(8,128)S(1)}, f32[32,128]{1,0:T(8,128)S(1)}, u32[]{:S(2)}, u32[]{:S(2)}) collective-permute-start(f32[32,128]{1,0:T(8,128)S(1)} %half.1.after_ref.own_ref), channel_id=1, source_target_pairs={{0,512},{64,576},{128,640},{192,704},{256,768},{320,832},{384,896}... | collective-permute-start | bytes 49160 | tf_op jit(solution)/shard_map/ppermute | solution.py:262
  28.6 0.7 copy-start.8
  81.2 8.7 %collective-permute-start.1 = (f32[32,128]{1,0:T(8,128)S(1)}, f32[32,128]{1,0:T(8,128)S(1)}, u32[]{:S(2)}, u32[]{:S(2)}) collective-permute-start(f32[32,128]{1,0:T(8,128)S(1)} %by_branch.1.after_ref.own_ref), channel_id=1, source_target_pairs={{0,512},{64,576},{128,640},{192,704},{256,768},{320,832},{384,896}... | collective-permute-start | bytes 49160 | tf_op jit(solution)/shard_map/ppermute | solution.py:302
  87.2 12.2 %copy-start.4 = (bf16[512,128]{1,0:T(8,128)(2,1)S(1)}, bf16[512,128]{1,0:T(8,128)(2,1)}, u32[]{:S(2)}) copy-start(bf16[512,128]{1,0:T(8,128)(2,1)} %bv_ref.1) | copy-start | bytes 393220
  89.9 9.5 %copy-start.3 = (bf16[512,128]{1,0:T(8,128)(2,1)S(1)}, bf16[512,128]{1,0:T(8,128)(2,1)}, u32[]{:S(2)}) copy-start(bf16[512,128]{1,0:T(8,128)(2,1)} %bk_ref.1) | copy-start | bytes 393220
  89.9 9.5 %copy-start.1 = (bf16[512,128]{1,0:T(8,128)(2,1)S(1)}, bf16[512,128]{1,0:T(8,128)(2,1)}, u32[]{:S(2)}) copy-start(bf16[512,128]{1,0:T(8,128)(2,1)} %tk_ref.1) | copy-start | bytes 393220
  89.9 9.5 %copy-start.2 = (bf16[512,128]{1,0:T(8,128)(2,1)S(1)}, bf16[512,128]{1,0:T(8,128)(2,1)}, u32[]{:S(2)}) copy-start(bf16[512,128]{1,0:T(8,128)(2,1)} %tv_ref.1) | copy-start | bytes 393220
